TPU v7x, 256 devices: a whole 4x4x8 slice. The times are simulated.
256 devices in a mesh: ctx: 32 (over x_hi, z, core), head: 4 (over y), video: 2 (over x_lo).
Axes of the slice: x: 4 (x_hi: 2, x_lo: 2; x = x_hi * 2 + x_lo), y: 4, z: 8, core: 2. Of those that a mesh axis runs over, the one named last changes fastest.
Arguments:
- queries: bfloat16 [2, 256, 3584], P('video', 'ctx', 'head'), may hold values from -6 to 6
- keys: bfloat16 [2, 4096, 512], P('video', 'ctx', 'head'), may hold values from -6 to 6
- values: bfloat16 [2, 4096, 512], P('video', 'ctx', 'head'), may hold values from -6 to 6
- dout: bfloat16 [2, 256, 3584], P('video', 'ctx', 'head'), may hold values from -192 to 192
- lengths: int32 [2], P('video'), may hold values from 8 to 32, as said below
- owner: int32 [2, 32], P('video', 'ctx'), may hold values from 0 to 31, as said below
- enc_rows: bfloat16 [2, 8192, 3584], P('video', 'ctx'), may hold values from -1.5 to 1.5
- w_kv: bfloat16 [3584, 1024], P(None, 'head'), may hold values from -0.09375 to 0.09375
Outputs:
- dq: bfloat16 [2, 256, 3584], P('video', 'ctx', 'head')
- enc_grad: bfloat16 [2, 8192, 3584], P('video', 'ctx', 'head')
- weight_grad: float32 [3584, 1024], P(('ctx', 'video'), 'head')
Inputs may be any that keep to these rules, and one draw needn't show every extreme that they name: In every draw some video has lengths equal to 32. With P = 32 and c = b, owner[v, b] is (c - 1) mod P or (c + 1) mod P; in every video some owner receives all blocks of both neighbours, 2 blocks. In some video whose length is 32, the first block of index P - 1 is owned by 0.
All inputs are finite; a program needn't handle non-finite values.
Results may differ from a plain program's by a relative error of at most 0.009.
Values may be sent and summed in bfloat16 or wider, within the bound.
A program may use at most 64 MiB of HBM per device.

v0:
```python
import math

import jax
import jax.numpy as jnp
from jax import lax
from jax.sharding import PartitionSpec as P

HD = 128
BLOCK = 128


def sent_together(arrays, axis, dim, along):
    widths = [a.shape[along] for a in arrays]
    both = jnp.concatenate(arrays, axis=along)
    filled = lax.all_gather(both, axis, axis=dim, tiled=True)
    return tuple(jnp.split(filled, [sum(widths[:k]) for k in range(1, len(widths))], axis=along))


def copy_for_each(array, axis):
    size = lax.axis_size(axis)
    return lax.all_to_all(
        jnp.broadcast_to(array[None], (size, *array.shape)), axis, 0, 0, tiled=True
    )


def gathered_once(array, axis):
    leaves = jax.tree.leaves(array)
    sequence = sorted(range(len(leaves)), key=lambda k: -leaves[k].size)
    width = (1, *leaves[sequence[0]].shape)[-1]
    lines = [
        jnp.pad(leaves[k].reshape(-1), (0, -leaves[k].size % width)).reshape(-1, width)
        for k in sequence
    ]
    both, at, found = (copy_for_each(jnp.concatenate(lines), axis), 0, {})
    for k, line in zip(sequence, lines):
        slab = both[:, at : at + len(line)].reshape(len(both), -1)
        found[k] = slab[:, : leaves[k].size].reshape(-1, *leaves[k].shape)
        at += len(line)
    numbers = iter(range(len(leaves)))
    return jax.tree.map(lambda _: found[next(numbers)], array)


def combined_pairwise(pieces, combine):
    while len(jax.tree.leaves(pieces)[0]) > 1:
        pieces = jax.vmap(combine)(
            *(jax.tree.map(lambda part: part[side::2], pieces) for side in (0, 1))
        )
    return jax.tree.map(lambda part: part[0], pieces)


def joined_all(array, axis, combine):
    pieces = gathered_once(array, axis)
    return combined_pairwise(pieces, combine)


def split_up(array, dim, size):
    before, after = (array.shape[:dim], array.shape[dim + 1 :])
    return jnp.moveaxis(array.reshape(*before, size, -1, *after), dim, 0)


def sent_and_summed(array, axis, dim):
    blocks = split_up(array, dim, lax.axis_size(axis))
    arrived = lax.all_to_all(blocks, axis, split_axis=0, concat_axis=0, tiled=True)
    return arrived.sum(axis=0)


def shifted(block, axis, distance):
    devices = range(lax.axis_size(axis))
    route = [((i - distance) % len(devices), i) for i in devices]
    return lax.ppermute(block, axis, route)


def sent_and_summed_2(array, axis, dim):
    blocks = split_up(array, dim, lax.axis_size(axis))
    arrived = lax.all_to_all(blocks, axis, split_axis=0, concat_axis=0, tiled=True)
    return arrived.astype(jnp.float32).sum(axis=0)


def combine_stats(earlier, later):
    upper = jnp.maximum(earlier[0], later[0])
    scale_one = jnp.exp(earlier[0] - upper)
    scale_two = jnp.exp(later[0] - upper)
    return (
        upper,
        earlier[1] * scale_one + later[1] * scale_two,
        earlier[2] * scale_one + later[2] * scale_two,
    )


def local_scores(query_rows, dout_rows, key_local, value_local):
    factor = 1.0 / math.sqrt(HD)
    scores = (
        jnp.einsum("rd,kd->rk", query_rows, key_local, preferred_element_type=jnp.float32) * factor
    )
    grad_prob = jnp.einsum("rd,kd->rk", dout_rows, value_local, preferred_element_type=jnp.float32)
    return (scores, grad_prob)


def local_stats(scores, grad_prob, key_valid):
    masked = jnp.where(key_valid[None, :], scores, -1e30)
    row_max = jnp.max(masked, axis=1)
    exp_terms = jnp.where(key_valid[None, :], jnp.exp(masked - row_max[:, None]), 0.0)
    return (row_max, jnp.sum(exp_terms, axis=1), jnp.sum(exp_terms * grad_prob, axis=1))


def backward_rows(scores, grad_prob, key_valid, stats, query_rows, dout_rows, key_local):
    factor = 1.0 / math.sqrt(HD)
    masked = jnp.where(key_valid[None, :], scores, -1e30)
    attention = (
        jnp.where(key_valid[None, :], jnp.exp(masked - stats[0][:, None]), 0.0) / stats[1][:, None]
    )
    grad_score = attention * (grad_prob - (stats[2] / stats[1])[:, None])
    attention_low = attention.astype(jnp.bfloat16)
    score_low = grad_score.astype(jnp.bfloat16)
    query_grad = jnp.dot(score_low, key_local, preferred_element_type=jnp.float32) * factor
    key_grad = (
        jnp.einsum("rk,rd->kd", score_low, query_rows, preferred_element_type=jnp.float32) * factor
    )
    value_grad = jnp.einsum(
        "rk,rd->kd", attention_low, dout_rows, preferred_element_type=jnp.float32
    )
    return (query_grad, key_grad, value_grad)


def per_device(queries, keys, values, dout, lengths, owner, enc_rows, w_kv):
    ctx_count = lax.axis_size("ctx")
    ctx_place = lax.axis_index("ctx")
    my_queries = queries[0]
    my_dout = dout[0]
    key_local = keys[0]
    value_local = values[0]
    vis_rows = key_local.shape[0]
    group_heads = my_queries.shape[1] // HD
    text_rows = my_queries.shape[0] * ctx_count
    positions = ctx_place * vis_rows + jnp.arange(vis_rows, dtype=jnp.int32)
    key_valid = positions // BLOCK < lengths[0]
    all_queries, all_dout = sent_together((my_queries, my_dout), "ctx", 0, 1)
    query_rows = all_queries.reshape(text_rows * group_heads, HD)
    dout_rows = all_dout.reshape(text_rows * group_heads, HD)
    scores, grad_prob = local_scores(query_rows, dout_rows, key_local, value_local)
    partial_stats = local_stats(scores, grad_prob, key_valid)
    stats = joined_all((partial_stats[0], partial_stats[1], partial_stats[2]), "ctx", combine_stats)
    query_grad, key_grad, value_grad = backward_rows(
        scores, grad_prob, key_valid, stats, query_rows, dout_rows, key_local
    )
    query_grad = query_grad.reshape(text_rows, group_heads * HD)
    my_query_grad = sent_and_summed(query_grad, "ctx", 0).astype(jnp.bfloat16)
    slot_blocks = vis_rows // BLOCK
    key_value = (
        jnp.concatenate([key_grad, value_grad], axis=1)
        .astype(jnp.bfloat16)
        .reshape(slot_blocks, BLOCK, 2 * HD)
    )
    goes_next = (owner[0] == (ctx_place + 1) % ctx_count)[:, None, None]
    zero_blocks = jnp.zeros_like(key_value)
    from_before = shifted(jnp.where(goes_next, key_value, zero_blocks), "ctx", 1)
    from_after = shifted(jnp.where(goes_next, zero_blocks, key_value), "ctx", -1)
    routed = jnp.concatenate([from_before, from_after], axis=0).reshape(2 * vis_rows, 2 * HD)
    enc_local = enc_rows[0]
    weight_grad = sent_and_summed(
        jnp.einsum("rd,rc->dc", enc_local, routed, preferred_element_type=jnp.float32),
        ("ctx", "video"),
        0,
    )
    head_term = jnp.einsum("rc,dc->rd", routed, w_kv, preferred_element_type=jnp.float32)
    enc_grad = sent_and_summed_2(head_term.astype(jnp.bfloat16), "head", 1)
    return (my_query_grad[None], enc_grad.astype(jnp.bfloat16)[None], weight_grad)


def solution(mesh):
    placed = (
        P("video", "ctx", "head"),
        P("video", "ctx", "head"),
        P("video", "ctx", "head"),
        P("video", "ctx", "head"),
        P("video"),
        P("video", "ctx"),
        P("video", "ctx", None),
        P(None, "head"),
    )
    return jax.shard_map(
        per_device,
        mesh=mesh,
        in_specs=placed,
        out_specs=(
            P("video", "ctx", "head"),
            P("video", "ctx", "head"),
            P(("ctx", "video"), "head"),
        ),
        check_vma=False,
    )
```

profile of v0, /device:TPU:1, one launch (start us, length us, event | category | flops | bytes accessed | tf_op | source)
XLA Modules:
  0.0 288.1 jit_solution(14629975153109684181)
XLA Ops:
  2.2 48.5 %all_gather.3 = bf16[256,1792]{1,0:T(8,128)(2,1)S(1)} all-gather(bf16[8,1792]{1,0:T(8,128)(2,1)S(1)} %pad_maximum_fusion.2), channel_id=1, replica_groups=mesh['ctx'=32,'head'=4,'video'=2] {'ctx'}, dimensions={0}, use_global_device_ids=true | all-gather | bytes 946176 | tf_op jit(solution)/shard_map/all_gather | solution.py:15
  52.8 2.2 fusion.5
  56.1 4.4 %all-to-all-start = ((f32[32,3,1792]{2,1,0:T(4,128)}), f32[32,3,1792]{2,1,0:T(4,128)}, u32[]{:S(2)}, u32[]{:S(2)}) async-start(f32[32,3,1792]{2,1,0:T(4,128)} %broadcast_in_dim.62), calls=%async_computation | async-start | bytes 1835008 | tf_op jit(solution)/shard_map/all_to_all | solution.py:21
  61.2 24.6 %all-to-all-done = f32[32,3,1792]{2,1,0:T(4,128)} async-done(((f32[32,3,1792]{2,1,0:T(4,128)}), f32[32,3,1792]{2,1,0:T(4,128)}, u32[]{:S(2)}, u32[]{:S(2)}) %all-to-all-start) | async-done | bytes 688160 | tf_op jit(solution)/shard_map/all_to_all | solution.py:21
  85.8 3.4 %fusion.16 = (f32[32,1,1792]{2,1,0:T(1,128)S(1)}, f32[32,1,1792]{2,1,0:T(1,128)}, f32[32,1,1792]{2,1,0:T(1,128)}) fusion(f32[32,3,1792]{2,1,0:T(4,128)} %all-to-all-done), kind=kLoop, calls=%fused_computation.64 | loop fusion | bytes 1376256 | tf_op jit(solution)/shard_map/slice | solution.py:36
  90.6 1.8 copy_bitcast_fusion
  94.1 1.6 multiply_add_fusion
  97.0 1.5 slice.131
  98.6 1.5 slice.130
  100.1 1.6 multiply_add_fusion.2
  101.7 1.4 slice.111
  103.1 1.4 slice.110
  104.5 1.4 slice.133
  106.0 1.4 slice.132
  107.4 1.4 multiply_add_fusion.4
  114.3 1.6 slice.118
  115.9 1.6 slice.117
  117.5 1.6 multiply_add_fusion.1
  124.5 1.5 fusion.3
  127.1 4.3 %collective-permute-start = (bf16[1,128,256]{1,2,0:T(8,128)(2,1)S(1)}, bf16[1,128,256]{1,2,0:T(8,128)(2,1)S(1)}, u32[]{:S(2)}, u32[]{:S(2)}) collective-permute-start(bf16[1,128,256]{1,2,0:T(8,128)(2,1)S(1)} %get-tuple-element.21), channel_id=1, source_target_pairs={{248,0},{0,8},{8,16},{16,24},{24,32},{32,40},{40,48},{48,56},{56,6... | collective-permute-start | bytes 196616 | tf_op jit(solution)/shard_map/ppermute | solution.py:70
  132.7 2.7 collective-permute-done.1
  137.6 4.5 %all-to-all-start.2 = ((bf16[4,256,896]{2,1,0:T(8,128)(2,1)}), bf16[4,256,896]{2,1,0:T(8,128)(2,1)}, u32[]{:S(2)}, u32[]{:S(2)}) async-start(bf16[4,256,896]{2,1,0:T(8,128)(2,1)} %bitcast.59), calls=%async_computation.2 | async-start | bytes 3670016 | tf_op jit(solution)/shard_map/all_to_all | solution.py:75
  143.4 1.5 copy.23
  146.0 18.0 %all-to-all-done.2 = bf16[4,256,896]{2,1,0:T(8,128)(2,1)} async-done(((bf16[4,256,896]{2,1,0:T(8,128)(2,1)}), bf16[4,256,896]{2,1,0:T(8,128)(2,1)}, u32[]{:S(2)}, u32[]{:S(2)}) %all-to-all-start.2) | async-done | bytes 1835040 | tf_op jit(solution)/shard_map/all_to_all | solution.py:75
  164.1 6.2 %all-to-all-start.1 = ((f32[32,8,896]{2,1,0:T(8,128)}), f32[32,8,896]{2,1,0:T(8,128)S(1)}, u32[]{:S(2)}, u32[]{:S(2)}) async-start(f32[32,8,896]{2,1,0:T(8,128)} %reshape_reshape.3), calls=%async_computation.1 | async-start | bytes 1835008 | tf_op jit(solution)/shard_map/all_to_all | solution.py:63
  170.3 4.0 %convolution_bitcast_fusion = f32[3584,256]{0,1:T(8,128)} fusion(bf16[256,256]{1,0:T(8,128)(2,1)S(1)} %bitcast.62, bf16[1,256,3584]{2,1,0:T(8,128)(2,1)} %param.14), kind=kOutput, calls=%fused_computation | convolution fusion | flops 469762048 | bytes 5636096 | tf_op jit(solution)/shard_map/rd,rc->dc/dot_general | solution.py:161
  174.3 5.1 %copy.26 = f32[3584,256]{1,0:T(8,128)} copy(f32[3584,256]{0,1:T(8,128)} %convolution_bitcast_fusion) | data formatting | bytes 7340032 | tf_op jit(solution)/shard_map/rd,rc->dc/dot_general | solution.py:161
  179.4 16.1 %all-to-all-done.1 = f32[32,8,896]{2,1,0:T(8,128)S(1)} async-done(((f32[32,8,896]{2,1,0:T(8,128)}), f32[32,8,896]{2,1,0:T(8,128)S(1)}, u32[]{:S(2)}, u32[]{:S(2)}) %all-to-all-start.1) | async-done | bytes 917536 | tf_op jit(solution)/shard_map/all_to_all | solution.py:63
  195.5 7.5 %all-to-all-start.3 = ((f32[64,56,256]{2,1,0:T(8,128)}), f32[64,56,256]{2,1,0:T(8,128)}, u32[]{:S(2)}, u32[]{:S(2)}) async-start(f32[64,56,256]{2,1,0:T(8,128)} %bitcast.58), calls=%async_computation.3 | async-start | bytes 7340032 | tf_op jit(solution)/shard_map/all_to_all | solution.py:63
  203.0 2.7 reduce_sum.51
  206.3 78.9 %all-to-all-done.3 = f32[64,56,256]{2,1,0:T(8,128)} async-done(((f32[64,56,256]{2,1,0:T(8,128)}), f32[64,56,256]{2,1,0:T(8,128)}, u32[]{:S(2)}, u32[]{:S(2)}) %all-to-all-start.3) | async-done | bytes 3670048 | tf_op jit(solution)/shard_map/all_to_all | solution.py:63
  285.2 2.9 reduce_sum.52
  (66 shorter events, 26.7 us)
Async XLA Ops:
  0.6 134.9 %copy-start = (bf16[3584,256]{1,0:T(8,128)(2,1)S(1)}, bf16[3584,256]{1,0:T(8,128)(2,1)}, u32[]{:S(2)}) copy-start(bf16[3584,256]{1,0:T(8,128)(2,1)} %param.15) | copy-start | bytes 5505028
  50.6 1.8 copy-start.5
  50.7 2.1 copy-start.7
  52.4 2.6 copy-start.8
  56.1 29.7 %all-to-all-start = ((f32[32,3,1792]{2,1,0:T(4,128)}), f32[32,3,1792]{2,1,0:T(4,128)}, u32[]{:S(2)}, u32[]{:S(2)}) async-start(f32[32,3,1792]{2,1,0:T(4,128)} %broadcast_in_dim.62), calls=%async_computation | async-start | bytes 1835008 | tf_op jit(solution)/shard_map/all_to_all | solution.py:21
  92.4 0.7 copy-start.4
  124.5 1.6 copy-start.3
  124.5 1.6 copy-start.9
  126.3 0.8 copy-start.1
  127.1 5.6 %collective-permute-start = (bf16[1,128,256]{1,2,0:T(8,128)(2,1)S(1)}, bf16[1,128,256]{1,2,0:T(8,128)(2,1)S(1)}, u32[]{:S(2)}, u32[]{:S(2)}) collective-permute-start(bf16[1,128,256]{1,2,0:T(8,128)(2,1)S(1)} %get-tuple-element.21), channel_id=1, source_target_pairs={{248,0},{0,8},{8,16},{16,24},{24,32},{32,40},{40,48},{48,56},{56,6... | collective-permute-start | bytes 196616 | tf_op jit(solution)/shard_map/ppermute | solution.py:70
  131.4 4.0 %collective-permute-start.1 = (bf16[1,128,256]{1,2,0:T(8,128)(2,1)S(1)}, bf16[1,128,256]{1,2,0:T(8,128)(2,1)S(1)}, u32[]{:S(2)}, u32[]{:S(2)}) collective-permute-start(bf16[1,128,256]{1,2,0:T(8,128)(2,1)S(1)} %get-tuple-element.22), channel_id=1, source_target_pairs={{8,0},{16,8},{24,16},{32,24},{40,32},{48,40},{56,48},{64,56},{72,6... | collective-permute-start | bytes 196616 | tf_op jit(solution)/shard_map/ppermute | solution.py:70
  137.6 4.5 %copy-start.2 = (bf16[1792,128]{0,1:T(8,128)(2,1)S(1)}, bf16[1792,128]{0,1:T(8,128)(2,1)}, u32[]{:S(2)}) copy-start(bf16[1792,128]{0,1:T(8,128)(2,1)} %copy-done.1) | copy-start | bytes 1376260
  137.6 4.5 %copy-start.6 = (bf16[1,128,128]{2,1,0:T(8,128)(2,1)S(1)}, bf16[1,128,128]{2,1,0:T(8,128)(2,1)}, u32[]{:S(2)}) copy-start(bf16[1,128,128]{2,1,0:T(8,128)(2,1)} %param.9) | copy-start | bytes 98308
  137.6 26.4 %all-to-all-start.2 = ((bf16[4,256,896]{2,1,0:T(8,128)(2,1)}), bf16[4,256,896]{2,1,0:T(8,128)(2,1)}, u32[]{:S(2)}, u32[]{:S(2)}) async-start(bf16[4,256,896]{2,1,0:T(8,128)(2,1)} %bitcast.59), calls=%async_computation.2 | async-start | bytes 3670016 | tf_op jit(solution)/shard_map/all_to_all | solution.py:75
  164.1 31.4 %all-to-all-start.1 = ((f32[32,8,896]{2,1,0:T(8,128)}), f32[32,8,896]{2,1,0:T(8,128)S(1)}, u32[]{:S(2)}, u32[]{:S(2)}) async-start(f32[32,8,896]{2,1,0:T(8,128)} %reshape_reshape.3), calls=%async_computation.1 | async-start | bytes 1835008 | tf_op jit(solution)/shard_map/all_to_all | solution.py:63
  195.5 89.8 %all-to-all-start.3 = ((f32[64,56,256]{2,1,0:T(8,128)}), f32[64,56,256]{2,1,0:T(8,128)}, u32[]{:S(2)}, u32[]{:S(2)}) async-start(f32[64,56,256]{2,1,0:T(8,128)} %bitcast.58), calls=%async_computation.3 | async-start | bytes 7340032 | tf_op jit(solution)/shard_map/all_to_all | solution.py:63
where the time goes:
time: 292 us; the launch traced here: 288 us
  waiting for transfers between devices  142 us (49%)
  blocking collectives  48.5 us (17%)
  local copies, waits for them, and re-layouts  41.5 us (14%)
  starting transfers between devices  26.9 us (9%)
  other arithmetic  16.9 us (6%)
  matrix products  10.4 us (4%)
    all_to_all x2, waiting for transfers between devices, sent_and_summed(): lax.all_to_all(blocks, axis, split_axis=0, concat_axis=0, tiled=True)  95 us
    all_gather x1, blocking collectives, sent_together(): filled = lax.all_gather(both, axis, axis=dim, tiled=True)  48.5 us
    all_to_all x1, waiting for transfers between devices, copy_for_each(): lax.all_to_all(jnp.broadcast_to(array[None], (size, *array.shape)), axis,...  24.6 us
    slice x24, local copies, waits for them, and re-layouts, combined_pairwise(): part[side::2]  23 us
    all_to_all x1, waiting for transfers between devices, sent_and_summed_2(): lax.all_to_all(blocks, axis, split_axis=0, concat_axis=0, tiled=True)  18 us
    all_to_all x2, starting transfers between devices, sent_and_summed(): lax.all_to_all(blocks, axis, split_axis=0, concat_axis=0, tiled=True)  13.7 us
  transfers between devices with their start and end apart: 6, of which 6 were waited for; matrix products, arithmetic and copies ran while one was open for 6% of the time, Pallas kernels for 0%

commit v1 on v0

v1 whole, which is shorter than its diff:
```python
import math

import jax
import jax.numpy as jnp
from jax import lax
from jax.experimental import pallas as pl
from jax.experimental.pallas import tpu as pltpu
from jax.sharding import PartitionSpec as P

NZ = 8
NC = 32
NH = 4
HD = 128
BLK = 128
QPG = 7
PIECE = 56
F32 = jnp.float32
BF16 = jnp.bfloat16
MESH = pl.DeviceIdType.MESH


def each(start, stop, fn):
    def step(i, carry):
        fn(i)
        return carry

    lax.fori_loop(start, stop, step, 0)


def nt(a, b):
    return lax.dot_general(a, b, (((1,), (1,)), ((), ())), preferred_element_type=F32)


def tn(a, b):
    return lax.dot_general(a, b, (((0,), (0,)), ((), ())), preferred_element_type=F32)


def kernel(
    q_ref, k_ref, v_ref, do_ref, len_ref, own_ref, enc_ref, w_ref,
    dq_ref, eg_ref, wg_ref,
    qv, dov, qg, kb, vb, encv, enct, encb, wb, st, cs, es, dp,
    dkvp, dkvr, dkvf, dkvg, hg, dqp, dqr, egs, wgs, wgr,
    lsem, q_s, q_r, kv_s, kv_r, st_s, st_r, dq_s, dq_r, rs_s, rs_r,
    gx_s, gx_r, gc_s, gc_r, e_s, e_r, w_s, w_r, h_s, h_r, o_s, o_r, wg_s, wg_r,
):
    factor = 1.0 / math.sqrt(HD)
    c = lax.axis_index("ctx")
    h = lax.axis_index("head")
    v = lax.axis_index("video")
    xh, z, k = lax.div(c, 2 * NZ), lax.rem(lax.div(c, 2), NZ), lax.rem(c, 2)
    xo, ko = 1 - xh, 1 - k
    c_next, c_prev = lax.rem(c + 1, NC), lax.rem(c + NC - 1, NC)
    c_cross = lax.rem(c + 2 * k - 1 + NC, NC)
    zt, xt = lax.rem(lax.div(c_cross, 2), NZ), lax.div(c_cross, 2 * NZ)

    def cid(a, b, d):
        return (a * NZ + b) * 2 + d

    def at(ctx, head, video):
        return {"ctx": ctx, "head": head, "video": video}

    def remote(src, dst, ssem, rsem, dev):
        return pltpu.make_async_remote_copy(
            src_ref=src, dst_ref=dst, send_sem=ssem, recv_sem=rsem,
            device_id=dev, device_id_type=MESH,
        )

    here = at(c, h, v)

    def zpeer(j):
        return lax.rem(z + j, NZ)

    def ppeer(d):
        return (
            lax.rem(xh + lax.div(d, 4), 2),
            lax.rem(k + lax.rem(lax.div(d, 2), 2), 2),
            lax.rem(v + lax.rem(d, 2), 2),
        )

    def bid(a, b, d):
        return a * 4 + b * 2 + d

    barrier = pltpu.get_barrier_semaphore()

    def signal(dev):
        pl.semaphore_signal(barrier, inc=1, device_id=dev, device_id_type=MESH)

    each(1, NZ, lambda j: signal(at(cid(xh, zpeer(j), k), h, v)))

    def sig_plane(d):
        a, b, e = ppeer(d)
        signal(at(cid(a, z, b), h, e))

    each(1, 8, sig_plane)

    def sig_cross(d):
        a, b, e = ppeer(d)
        signal(at(lax.rem(cid(a, z, b) + 2 * b - 1 + NC, NC), h, e))

    each(0, 8, sig_cross)
    each(1, NH, lambda j: signal(at(c, lax.rem(h + j, NH), v)))

    own4 = xh * 2 + k
    wrows = pl.ds(pl.multiple_of(h * 896, 128), 896)
    loads = [
        pltpu.make_async_copy(q_ref, qv, lsem.at[0]),
        pltpu.make_async_copy(do_ref, dov, lsem.at[1]),
        pltpu.make_async_copy(k_ref, kb.at[own4], lsem.at[2]),
        pltpu.make_async_copy(v_ref, vb.at[own4], lsem.at[3]),
        pltpu.make_async_copy(enc_ref, encv, lsem.at[4]),
        pltpu.make_async_copy(w_ref.at[wrows], wb.at[h], lsem.at[5]),
    ]
    for load in loads:
        load.start()
    loads[0].wait()
    loads[1].wait()
    pad = jnp.zeros((8, HD), F32)
    for side, ref in ((0, qv), (1, dov)):
        rows = ref[...].astype(F32)
        parts = [rows[:, g * HD : (g + 1) * HD] for g in range(QPG)] + [pad]
        qg[z, side] = jnp.concatenate(parts, axis=0).astype(BF16)

    pl.semaphore_wait(barrier, 25)

    def q_copy(j):
        zd = zpeer(j)
        return remote(qg.at[z], qg.at[z], q_s.at[zd], q_r.at[z], at(cid(xh, zd, k), h, v))

    each(1, NZ, lambda j: q_copy(j).start())

    def kv_peer(d):
        return lax.rem(xh + lax.div(d, 2), 2), lax.rem(k + lax.rem(d, 2), 2)

    def kv_copy(d, side):
        a, b = kv_peer(d)
        src, dst = ((k_ref, kb), (v_ref, vb))[side]
        return remote(
            src, dst.at[own4], kv_s.at[side, a * 2 + b], kv_r.at[side, own4], at(cid(a, z, b), h, v)
        )

    for side in (0, 1):
        each(1, 4, lambda d: kv_copy(d, side).start())

    def w_copy(j):
        hd = lax.rem(h + j, NH)
        rows = pl.ds(pl.multiple_of(hd * 896, 128), 896)
        return remote(w_ref.at[rows], wb.at[h], w_s.at[hd], w_r.at[h], at(c, hd, v))

    each(1, NH, lambda j: w_copy(j).start())

    row = lax.broadcasted_iota(jnp.int32, (1024, 896), 0)
    col = lax.broadcasted_iota(jnp.int32, (1024, 896), 1)
    inner_row = lax.rem(row, 256)
    quarter = lax.div(row, 256)
    step_of = (
        (inner_row >= PIECE).astype(jnp.int32)
        + (inner_row >= 2 * PIECE).astype(jnp.int32)
        + (inner_row >= 3 * PIECE).astype(jnp.int32)
    )
    source = step_of * (4 * PIECE) + quarter * PIECE + inner_row - step_of * PIECE
    pick = jnp.where((col == source) & (inner_row < 4 * PIECE), 1.0, 0.0).astype(BF16)
    loads[4].wait()
    for g in range(4):
        turned = nt(pick, encv[:, g * 896 : (g + 1) * 896]).astype(BF16)
        for slot in (0, 1):
            for t in range(4):
                enct[slot, g // 2, t, (g % 2) * 256 : (g % 2) * 256 + 256] = turned[
                    t * 256 : (t + 1) * 256, slot * 128 : (slot + 1) * 128
                ]

    def lanes(side):
        return pl.ds(side * 128, 128)

    b_same, b_cross = bid(xh, ko, v), bid(xt, ko, v)

    def enc_same(d):
        a, b, e = ppeer(d)
        return remote(
            enct.at[ko, a, b * 2 + e], encb.at[b_same, :, lanes(0)],
            e_s.at[0, d], e_r.at[0, b_same], at(cid(a, z, b), h, e),
        )

    def enc_cross(d):
        a, b, e = ppeer(d)
        return remote(
            enct.at[k, a, b * 2 + e], encb.at[b_cross, :, lanes(1)],
            e_s.at[1, d], e_r.at[1, b_cross], at(cid(a, zt, b), h, e),
        )

    enc_own = pltpu.make_async_copy(
        enct.at[ko, xh, k * 2 + v], encb.at[b_same, :, lanes(0)], lsem.at[6]
    )
    each(1, 8, lambda d: enc_same(d).start())
    enc_own.start()

    def q_arrived(j):
        zs = zpeer(j)
        remote(qg.at[zs], qg.at[zs], q_s.at[zs], q_r.at[zs], here).wait_recv()

    def kv_arrived(d):
        a, b = kv_peer(d)
        i = a * 2 + b
        remote(k_ref, kb.at[i], kv_s.at[0, i], kv_r.at[0, i], here).wait_recv()
        remote(v_ref, vb.at[i], kv_s.at[1, i], kv_r.at[1, i], here).wait_recv()

    loads[2].wait()
    loads[3].wait()
    each(1, 4, kv_arrived)
    each(1, NZ, q_arrived)
    keys = kb[...].reshape(512, HD)
    queries = qg[:, 0].reshape(512, HD)
    dout = qg[:, 1].reshape(512, HD)
    block = lax.div(lax.broadcasted_iota(jnp.int32, (512, 512), 0), BLK)
    place = lax.div(block, 2) * (2 * NZ) + z * 2 + lax.rem(block, 2)
    valid = place < len_ref[0]
    masked = jnp.where(valid, nt(keys, queries) * factor, -1e30)
    top = jnp.max(masked, axis=0, keepdims=True)
    terms = jnp.where(valid, jnp.exp(masked - top), 0.0)
    grad_prob = nt(vb[...].reshape(512, HD), dout)
    es[...] = terms
    dp[...] = grad_prob
    total = jnp.sum(terms, axis=0, keepdims=True)
    inner = jnp.sum(terms * grad_prob, axis=0, keepdims=True)
    for n, value in enumerate((top, total, inner)):
        for t in range(4):
            st[z, n * 4 + t : n * 4 + t + 1, :] = value[:, t * 128 : (t + 1) * 128]

    def st_copy(j):
        zd = zpeer(j)
        return remote(st.at[z], st.at[z], st_s.at[zd], st_r.at[z], at(cid(xh, zd, k), h, v))

    def st_arrived(j):
        zs = zpeer(j)
        remote(st.at[zs], st.at[zs], st_s.at[zs], st_r.at[zs], here).wait_recv()

    each(1, NZ, lambda j: st_copy(j).start())
    each(0, 8, lambda d: enc_cross(d).start())
    each(1, NZ, st_arrived)
    tops, totals, inners = st[:, 0:4, :], st[:, 4:8, :], st[:, 8:12, :]
    upper = jnp.max(tops, axis=0)
    scales = jnp.exp(tops - upper[None])
    sum_total = jnp.sum(totals * scales, axis=0)
    sum_inner = jnp.sum(inners * scales, axis=0)
    cs[0:4, :] = jnp.exp(st[z, 0:4, :] - upper) / sum_total
    cs[4:8, :] = sum_inner / sum_total
    scale = jnp.concatenate([cs[t : t + 1, :] for t in range(4)], axis=1)
    ratio = jnp.concatenate([cs[t : t + 1, :] for t in range(4, 8)], axis=1)
    attention = es[...] * scale
    score_low = (attention * (dp[...] - ratio)).astype(BF16)
    attention_low = attention.astype(BF16)
    key_grad = jnp.dot(score_low, queries, preferred_element_type=F32) * factor
    value_grad = jnp.dot(attention_low, dout, preferred_element_type=F32)
    key_value = jnp.concatenate([key_grad, value_grad], axis=1).reshape(4, BLK, 256)
    dkvf[...] = key_value
    dkvp[...] = key_value.astype(BF16)

    def rs_copy(d):
        a, b = kv_peer(d)
        i = a * 2 + b
        return remote(dkvp.at[i], dkvr.at[own4], rs_s.at[i], rs_r.at[own4], at(cid(a, z, b), h, v))

    def rs_arrived(d):
        a, b = kv_peer(d)
        i = a * 2 + b
        remote(dkvp.at[i], dkvr.at[i], rs_s.at[i], rs_r.at[i], here).wait_recv()

    each(1, 4, lambda d: rs_copy(d).start())

    dqp[...] = tn(score_low, keys).reshape(NZ, 64, HD).astype(BF16)

    def dq_copy(j):
        zd = zpeer(j)
        return remote(dqp.at[zd], dqr.at[z], dq_s.at[zd], dq_r.at[z], at(cid(xh, zd, k), h, v))

    def dq_arrived(j):
        zs = zpeer(j)
        remote(dqp.at[zs], dqr.at[zs], dq_s.at[zs], dq_r.at[zs], here).wait_recv()

    each(1, NZ, lambda j: dq_copy(j).start())
    each(1, 4, rs_arrived)
    mine = dkvf[own4]
    for d in range(1, 4):
        a, b = kv_peer(d)
        mine = mine + dkvr[a * 2 + b].astype(F32)
    mine = mine.astype(BF16)
    owner = own_ref[0, 0]
    b_me = bid(xh, k, v)
    to_same = jnp.where(jnp.full((16, 256), owner, jnp.int32) == c + 1 - 2 * k, 1.0, 0.0)
    dkvg[b_me, 0:128, :] = mine
    dkvg[b_me, 128:144, :] = to_same.astype(BF16)
    hg[h] = mine

    def gx_peer(d):
        return lax.rem(xh + lax.div(d, 2), 2), lax.rem(v + lax.rem(d, 2), 2)

    def gx_copy(d):
        a, e = gx_peer(d)
        return remote(
            dkvg.at[b_me], dkvg.at[b_me], gx_s.at[a * 2 + e], gx_r.at[xh * 2 + v],
            at(cid(a, z, k), h, e),
        )

    def gc_copy(d):
        a, e = gx_peer(d)
        i = bid(a, k, e)
        return remote(
            dkvg.at[i], dkvg.at[i], gc_s.at[a * 2 + e], gc_r.at[a * 2 + e], at(cid(xh, z, ko), h, v)
        )

    def h_copy(j):
        hd = lax.rem(h + j, NH)
        return remote(hg.at[h], hg.at[h], h_s.at[hd], h_r.at[h], at(c, hd, v))

    each(1, 4, lambda d: gx_copy(d).start())
    each(1, NH, lambda j: h_copy(j).start())
    gc_copy(0).start()

    def forward(d):
        a, e = gx_peer(d)
        i = bid(a, k, e)
        remote(
            dkvg.at[i], dkvg.at[i], gx_s.at[a * 2 + e], gx_r.at[a * 2 + e], here
        ).wait_recv()
        gc_copy(d).start()

    each(1, 4, forward)

    def h_arrived(j):
        hs = lax.rem(h + j, NH)
        remote(hg.at[hs], hg.at[hs], h_s.at[hs], h_r.at[hs], here).wait_recv()

    def w_arrived(j):
        hs = lax.rem(h + j, NH)
        remote(w_ref.at[wrows], wb.at[hs], w_s.at[hs], w_r.at[hs], here).wait_recv()

    loads[5].wait()
    each(1, NH, w_arrived)
    each(1, NH, h_arrived)
    summed = jnp.zeros((BLK, 896), F32)
    for g in range(NH):
        summed = summed + nt(hg[g], wb[g]).astype(BF16).astype(F32)
    owners = jnp.full((BLK, 896), owner, jnp.int32)
    egs[0] = jnp.where(owners == c_next, summed, 0.0).astype(BF16)
    egs[1] = jnp.where(owners == c_next, 0.0, summed).astype(BF16)
    out_next = remote(
        egs.at[0], eg_ref.at[pl.ds(0, 128)], o_s.at[0], o_r.at[0], at(c_next, h, v)
    )
    out_prev = remote(
        egs.at[1], eg_ref.at[pl.ds(128, 128)], o_s.at[1], o_r.at[1], at(c_prev, h, v)
    )
    out_next.start()
    out_prev.start()

    def gc_arrived(d):
        a, e = gx_peer(d)
        i = bid(a, ko, e)
        remote(dkvg.at[i], dkvg.at[i], gc_s.at[a * 2 + e], gc_r.at[a * 2 + e], here).wait_recv()

    def enc_arrived(side, a, b, e):
        i = bid(a, b, e)
        remote(
            enct.at[0, 0, 0], encb.at[i, :, lanes(side)], e_s.at[side, 0], e_r.at[side, i], here
        ).wait_recv()

    def same_arrived(d):
        a, b, e = ppeer(d)
        enc_arrived(0, a, 1 - b, e)

    each(0, 4, gc_arrived)
    enc_own.wait()
    each(1, 8, same_arrived)
    each(0, 8, lambda d: enc_arrived(1, *ppeer(d)))
    acc = jnp.zeros((512, 256), F32)
    for i in range(8):
        grads = dkvg[i, 0:128, :].astype(F32)
        flag = dkvg[i, 128:144, :].astype(F32)[0:1, :]
        both = jnp.concatenate([grads * flag, grads * (1.0 - flag)], axis=0).astype(BF16)
        acc = acc + jnp.dot(encb[i], both, preferred_element_type=F32)
    for t in range(NZ):
        first = (t // 4) * 256 + (t % 4) * PIECE
        wgs[t] = acc[first : first + 64].astype(BF16)

    def wg_copy(j):
        zd = zpeer(j)
        return remote(wgs.at[zd], wgr.at[z], wg_s.at[zd], wg_r.at[z], at(cid(xh, zd, k), h, v))

    def wg_arrived(j):
        zs = zpeer(j)
        remote(wgs.at[zs], wgr.at[zs], wg_s.at[zs], wg_r.at[zs], here).wait_recv()

    each(1, NZ, lambda j: wg_copy(j).start())

    each(1, NZ, dq_arrived)
    query_grad = dqp[z].astype(F32)
    for j in range(1, NZ):
        query_grad = query_grad + dqr[zpeer(j)].astype(F32)
    query_grad = query_grad * factor
    dq_ref[...] = jnp.concatenate(
        [query_grad[g * 8 : (g + 1) * 8] for g in range(QPG)], axis=1
    ).astype(BF16)

    each(1, NZ, wg_arrived)
    weight = wgs[z].astype(F32)
    for j in range(1, NZ):
        weight = weight + wgr[zpeer(j)].astype(F32)
    wg_ref[...] = weight[:PIECE]

    out_next.wait_recv()
    out_prev.wait_recv()
    each(1, NZ, lambda j: q_copy(j).wait_send())
    for side in (0, 1):
        each(1, 4, lambda d: kv_copy(d, side).wait_send())
    each(1, NH, lambda j: w_copy(j).wait_send())
    each(1, 8, lambda d: enc_same(d).wait_send())
    each(0, 8, lambda d: enc_cross(d).wait_send())
    each(1, NZ, lambda j: st_copy(j).wait_send())
    each(1, 4, lambda d: rs_copy(d).wait_send())
    each(1, NZ, lambda j: dq_copy(j).wait_send())
    each(1, 4, lambda d: gx_copy(d).wait_send())
    each(0, 4, lambda d: gc_copy(d).wait_send())
    each(1, NH, lambda j: h_copy(j).wait_send())
    out_next.wait_send()
    out_prev.wait_send()
    each(1, NZ, lambda j: wg_copy(j).wait_send())


def per_device(queries, keys, values, dout, lengths, owner, enc_rows, w_kv):
    dma = pltpu.SemaphoreType.DMA
    vmem = pltpu.VMEM
    hbm = pl.BlockSpec(memory_space=pl.ANY)
    smem = pl.BlockSpec(memory_space=pltpu.SMEM)
    out = pl.BlockSpec(memory_space=pltpu.VMEM)
    dq, eg, wg = pl.pallas_call(
        kernel,
        out_shape=(
            jax.ShapeDtypeStruct((8, 896), BF16),
            jax.ShapeDtypeStruct((256, 896), BF16),
            jax.ShapeDtypeStruct((PIECE, 256), F32),
        ),
        in_specs=[hbm, hbm, hbm, hbm, smem, smem, hbm, hbm],
        out_specs=(out, hbm, out),
        scratch_shapes=[
            vmem((8, 896), BF16),
            vmem((8, 896), BF16),
            vmem((NZ, 2, 64, HD), BF16),
            vmem((4, BLK, HD), BF16),
            vmem((4, BLK, HD), BF16),
            vmem((256, 3584), BF16),
            vmem((2, 2, 4, 512, 128), BF16),
            vmem((8, 512, 256), BF16),
            vmem((NH, 896, 256), BF16),
            vmem((NZ, 16, 128), F32),
            vmem((8, 128), F32),
            vmem((512, 512), F32),
            vmem((512, 512), F32),
            vmem((4, BLK, 256), BF16),
            vmem((4, BLK, 256), BF16),
            vmem((4, BLK, 256), F32),
            vmem((8, 144, 256), BF16),
            vmem((NH, BLK, 256), BF16),
            vmem((NZ, 64, HD), BF16),
            vmem((NZ, 64, HD), BF16),
            vmem((2, BLK, 896), BF16),
            vmem((NZ, 64, 256), BF16),
            vmem((NZ, 64, 256), BF16),
            dma((7,)),
            dma((NZ,)), dma((NZ,)),
            dma((2, 4)), dma((2, 4)),
            dma((NZ,)), dma((NZ,)),
            dma((NZ,)), dma((NZ,)),
            dma((4,)), dma((4,)),
            dma((4,)), dma((4,)),
            dma((4,)), dma((4,)),
            dma((2, 8)), dma((2, 8)),
            dma((NH,)), dma((NH,)),
            dma((NH,)), dma((NH,)),
            dma((2,)), dma((2,)),
            dma((NZ,)), dma((NZ,)),
        ],
        compiler_params=pltpu.CompilerParams(
            collective_id=0, has_side_effects=True, vmem_limit_bytes=60 * 1024 * 1024
        ),
    )(queries[0], keys[0], values[0], dout[0], lengths, owner, enc_rows[0], w_kv)
    return dq[None], eg[None], wg


def solution(mesh):
    placed = (
        P("video", "ctx", "head"),
        P("video", "ctx", "head"),
        P("video", "ctx", "head"),
        P("video", "ctx", "head"),
        P("video"),
        P("video", "ctx"),
        P("video", "ctx", None),
        P(None, "head"),
    )
    return jax.shard_map(
        per_device,
        mesh=mesh,
        in_specs=placed,
        out_specs=(
            P("video", "ctx", "head"),
            P("video", "ctx", "head"),
            P(("ctx", "video"), "head"),
        ),
        check_vma=False,
    )
```

time: 292 us -> 72.4 us (0.25); the launches traced: 288 us -> 72.1 us
  waiting for transfers between devices: 142 us -> 0 us
  Pallas kernels: 0 us -> 65.6 us
  blocking collectives: 48.5 us -> 0 us
  local copies, waits for them, and re-layouts: 41.5 us -> 4.58 us
  starting transfers between devices: 26.9 us -> 0 us
  other arithmetic: 16.9 us -> 0 us
  matrix products: 10.4 us -> 0 us
    all_to_all x4 -> x0, waiting for transfers between devices: 138 us -> none  [the longest x2 95 us: sent_and_summed(): lax.all_to_all(blocks, axis, split_axis=0, concat_axis=0, tiled=True)]
    pallas_call x0 -> x1, Pallas kernels: none -> 65.6 us  [per_device(): pl.pallas_call(kernel, out_shape=(jax.ShapeDtypeStruct((8, 896), BF16), j...]
    all_gather x1 -> x0, blocking collectives: 48.5 us -> none  [sent_together(): filled = lax.all_gather(both, axis, axis=dim, tiled=True)]
    slice x25 -> x0, local copies, waits for them, and re-layouts: 26.5 us -> none  [the longest x24 23 us: combined_pairwise(): part[side::2]]
    all_to_all x4 -> x0, starting transfers between devices: 22.6 us -> none  [the longest x2 13.7 us: sent_and_summed(): lax.all_to_all(blocks, axis, split_axis=0, concat_axis=0, tiled=True)]
    dot_general x7 -> x0, matrix products: 10.4 us -> none  [the longest x1 4.01 us: per_device(): jnp.einsum('rd,rc->dc', enc_local, routed, preferred_element_type=jnp.flo...]
    add x9 -> x0, other arithmetic: 9.65 us -> none  [the longest x4 5.44 us: combine_stats(): earlier[2] * scale_one + later[2] * scale_two]
    reduce_sum x3 -> x0, other arithmetic: 6.2 us -> none  [the longest x2 3.54 us: sent_and_summed(): return arrived.sum(axis=0)]
  transfers between devices with their start and end apart: 6 -> 0, of which waited for: 6 -> 0; matrix products, arithmetic and copies ran while one was open for 6% -> 0% of each run, Pallas kernels for 0% -> 0%
where the time goes in v1:
time: 72.4 us; the launch traced here: 72.1 us
  Pallas kernels  65.6 us (91%)
  local copies, waits for them, and re-layouts  4.58 us (6%)
  between operations  1.93 us (3%)
    pallas_call x1, Pallas kernels, per_device(): pl.pallas_call(kernel, out_shape=(jax.ShapeDtypeStruct((8, 896), BF16), j...  65.6 us
    unnamed x3, local copies, waits for them, and re-layouts  4.58 us

profile of v1, /device:TPU:1, one launch (start us, length us, event | category | flops | bytes accessed | tf_op | source)
XLA Modules:
  0.0 72.1 jit_solution(18384145132997751064)
XLA Ops:
  1.9 65.6 %shard_map.103 = (bf16[8,896]{1,0:T(8,128)(2,1)}, bf16[256,896]{1,0:T(8,128)(2,1)}, f32[56,256]{1,0:T(8,128)}) custom-call(bf16[8,896]{1,0:T(8,128)(2,1)} %bitcast.11, bf16[128,128]{1,0:T(8,128)(2,1)} %bitcast.9, bf16[128,128]{1,0:T(8,128)(2,1)} %bitcast.10, bf16[8,896]{1,0:T(8,128)(2,1)} %bitcast.12, s32[1]{0:T(128)S(6)} %copy.14.len_ref, ...), custom_call_target="tpu_custom_call" | custom-call | tf_op jit(solution)/shard_map/pallas_call | solution.py:433
  67.5 1.3 %copy.16 = bf16[1,8,896]{2,1,0:T(8,128)(2,1)} copy(bf16[1,8,896]{2,1,0:T(8,128)(2,1)} %bitcast.13) | data formatting | bytes 28672
  68.8 1.8 %copy.17 = bf16[1,256,896]{2,1,0:T(8,128)(2,1)} copy(bf16[1,256,896]{2,1,0:T(8,128)(2,1)} %bitcast.8) | data formatting | bytes 917504
  70.7 1.4 %copy.18 = f32[56,256]{1,0:T(8,128)} copy(f32[56,256]{1,0:T(8,128)} %get-tuple-element.14) | data formatting | bytes 114688

commit v2 on v1

--- a/solution.py
+++ b/solution.py
@@ -38,20 +38,20 @@
 def kernel(
     q_ref, k_ref, v_ref, do_ref, len_ref, own_ref, enc_ref, w_ref,
     dq_ref, eg_ref, wg_ref,
-    qv, dov, qg, kb, vb, encv, enct, encb, wb, st, cs, es, dp,
+    qv, dov, qg, kb, vb, cand, encs, encb, wb, st, cs, es, dp,
     dkvp, dkvr, dkvf, dkvg, hg, dqp, dqr, egs, wgs, wgr,
     lsem, q_s, q_r, kv_s, kv_r, st_s, st_r, dq_s, dq_r, rs_s, rs_r,
-    gx_s, gx_r, gc_s, gc_r, e_s, e_r, w_s, w_r, h_s, h_r, o_s, o_r, wg_s, wg_r,
+    gx_s, gx_r, gc_s, gc_r, c_s, c_r, ex_s, ex_r, ey_s, ey_r,
+    w_s, w_r, wf_s, wf_r, h_s, h_r, o_s, o_r, wg_s, wg_r,
 ):
     factor = 1.0 / math.sqrt(HD)
     c = lax.axis_index("ctx")
     h = lax.axis_index("head")
     v = lax.axis_index("video")
     xh, z, k = lax.div(c, 2 * NZ), lax.rem(lax.div(c, 2), NZ), lax.rem(c, 2)
-    xo, ko = 1 - xh, 1 - k
+    ko = 1 - k
     c_next, c_prev = lax.rem(c + 1, NC), lax.rem(c + NC - 1, NC)
     c_cross = lax.rem(c + 2 * k - 1 + NC, NC)
-    zt, xt = lax.rem(lax.div(c_cross, 2), NZ), lax.div(c_cross, 2 * NZ)
 
     def cid(a, b, d):
         return (a * NZ + b) * 2 + d
@@ -69,6 +69,13 @@
 
     def zpeer(j):
         return lax.rem(z + j, NZ)
+
+    def far_first(fn):
+        def step(i):
+            half = lax.div(i + 1, 2)
+            fn(4 + half - 2 * half * lax.rem(i, 2))
+
+        each(0, NZ - 1, step)
 
     def ppeer(d):
         return (
@@ -93,11 +100,7 @@
 
     each(1, 8, sig_plane)
 
-    def sig_cross(d):
-        a, b, e = ppeer(d)
-        signal(at(lax.rem(cid(a, z, b) + 2 * b - 1 + NC, NC), h, e))
-
-    each(0, 8, sig_cross)
+    signal(at(c_cross, h, v))
     each(1, NH, lambda j: signal(at(c, lax.rem(h + j, NH), v)))
 
     own4 = xh * 2 + k
@@ -107,8 +110,7 @@
         pltpu.make_async_copy(do_ref, dov, lsem.at[1]),
         pltpu.make_async_copy(k_ref, kb.at[own4], lsem.at[2]),
         pltpu.make_async_copy(v_ref, vb.at[own4], lsem.at[3]),
-        pltpu.make_async_copy(enc_ref, encv, lsem.at[4]),
-        pltpu.make_async_copy(w_ref.at[wrows], wb.at[h], lsem.at[5]),
+        pltpu.make_async_copy(w_ref.at[wrows], wb.at[h], lsem.at[4]),
     ]
     for load in loads:
         load.start()
@@ -119,34 +121,6 @@
         rows = ref[...].astype(F32)
         parts = [rows[:, g * HD : (g + 1) * HD] for g in range(QPG)] + [pad]
         qg[z, side] = jnp.concatenate(parts, axis=0).astype(BF16)
-
-    pl.semaphore_wait(barrier, 25)
-
-    def q_copy(j):
-        zd = zpeer(j)
-        return remote(qg.at[z], qg.at[z], q_s.at[zd], q_r.at[z], at(cid(xh, zd, k), h, v))
-
-    each(1, NZ, lambda j: q_copy(j).start())
-
-    def kv_peer(d):
-        return lax.rem(xh + lax.div(d, 2), 2), lax.rem(k + lax.rem(d, 2), 2)
-
-    def kv_copy(d, side):
-        a, b = kv_peer(d)
-        src, dst = ((k_ref, kb), (v_ref, vb))[side]
-        return remote(
-            src, dst.at[own4], kv_s.at[side, a * 2 + b], kv_r.at[side, own4], at(cid(a, z, b), h, v)
-        )
-
-    for side in (0, 1):
-        each(1, 4, lambda d: kv_copy(d, side).start())
-
-    def w_copy(j):
-        hd = lax.rem(h + j, NH)
-        rows = pl.ds(pl.multiple_of(hd * 896, 128), 896)
-        return remote(w_ref.at[rows], wb.at[h], w_s.at[hd], w_r.at[h], at(c, hd, v))
-
-    each(1, NH, lambda j: w_copy(j).start())
 
     row = lax.broadcasted_iota(jnp.int32, (1024, 896), 0)
     col = lax.broadcasted_iota(jnp.int32, (1024, 896), 1)
@@ -159,39 +133,61 @@
     )
     source = step_of * (4 * PIECE) + quarter * PIECE + inner_row - step_of * PIECE
     pick = jnp.where((col == source) & (inner_row < 4 * PIECE), 1.0, 0.0).astype(BF16)
-    loads[4].wait()
-    for g in range(4):
-        turned = nt(pick, encv[:, g * 896 : (g + 1) * 896]).astype(BF16)
-        for slot in (0, 1):
-            for t in range(4):
-                enct[slot, g // 2, t, (g % 2) * 256 : (g % 2) * 256 + 256] = turned[
-                    t * 256 : (t + 1) * 256, slot * 128 : (slot + 1) * 128
-                ]
-
-    def lanes(side):
-        return pl.ds(side * 128, 128)
-
-    b_same, b_cross = bid(xh, ko, v), bid(xt, ko, v)
-
-    def enc_same(d):
-        a, b, e = ppeer(d)
+
+    pl.semaphore_wait(barrier, 18)
+
+    def q_copy(j):
+        zd = zpeer(j)
+        return remote(qg.at[z], qg.at[z], q_s.at[zd], q_r.at[z], at(cid(xh, zd, k), h, v))
+
+    far_first(lambda j: q_copy(j).start())
+
+    def kv_peer(d):
+        return lax.rem(xh + lax.div(d, 2), 2), lax.rem(k + lax.rem(d, 2), 2)
+
+    def kv_copy(d, side):
+        a, b = kv_peer(d)
+        src, dst = ((k_ref, kb), (v_ref, vb))[side]
         return remote(
-            enct.at[ko, a, b * 2 + e], encb.at[b_same, :, lanes(0)],
-            e_s.at[0, d], e_r.at[0, b_same], at(cid(a, z, b), h, e),
+            src, dst.at[own4], kv_s.at[side, a * 2 + b], kv_r.at[side, own4], at(cid(a, z, b), h, v)
         )
 
-    def enc_cross(d):
-        a, b, e = ppeer(d)
-        return remote(
-            enct.at[k, a, b * 2 + e], encb.at[b_cross, :, lanes(1)],
-            e_s.at[1, d], e_r.at[1, b_cross], at(cid(a, zt, b), h, e),
-        )
-
-    enc_own = pltpu.make_async_copy(
-        enct.at[ko, xh, k * 2 + v], encb.at[b_same, :, lanes(0)], lsem.at[6]
-    )
-    each(1, 8, lambda d: enc_same(d).start())
-    enc_own.start()
+    for side in (0, 1):
+        each(1, 4, lambda d: kv_copy(d, side).start())
+
+    def cand_copy(side):
+        slot, ctx = ((ko, cid(xh, z, ko)), (k, c_cross))[side]
+        rows = pl.ds(pl.multiple_of(slot * BLK + h * 32, 32), 32)
+        return remote(enc_ref.at[rows], cand.at[side], c_s.at[side], c_r.at[side], at(ctx, h, v))
+
+    cand_copy(0).start()
+    cand_copy(1).start()
+
+    half_rows = pl.ds(pl.multiple_of(k * 448, 64), 448)
+    rest_rows = pl.ds(pl.multiple_of(ko * 448, 64), 448)
+
+    def w_copy(j):
+        hd = lax.rem(h + j, NH)
+        rows = pl.ds(pl.multiple_of(hd * 896 + k * 448, 64), 448)
+        return remote(w_ref.at[rows], wb.at[h, half_rows], w_s.at[hd], w_r.at[h], at(c, hd, v))
+
+    def w_forward(j):
+        hs = lax.rem(h + j, NH)
+        part = wb.at[hs, half_rows]
+        remote(part, part, w_s.at[hs], w_r.at[hs], here).wait_recv()
+        w_pass(j).start()
+
+    def w_pass(j):
+        hs = lax.rem(h + j, NH)
+        part = wb.at[hs, half_rows]
+        return remote(part, part, wf_s.at[hs], wf_r.at[hs], at(cid(xh, z, ko), h, v))
+
+    def w_arrived(j):
+        hs = lax.rem(h + j, NH)
+        part = wb.at[hs, rest_rows]
+        remote(part, part, wf_s.at[hs], wf_r.at[hs], here).wait_recv()
+
+    each(1, NH, lambda j: w_copy(j).start())
 
     def q_arrived(j):
         zs = zpeer(j)
@@ -233,8 +229,43 @@
         zs = zpeer(j)
         remote(st.at[zs], st.at[zs], st_s.at[zs], st_r.at[zs], here).wait_recv()
 
-    each(1, NZ, lambda j: st_copy(j).start())
-    each(0, 8, lambda d: enc_cross(d).start())
+    far_first(lambda j: st_copy(j).start())
+
+    owner = own_ref[0, 0]
+    b_me = bid(xh, k, v)
+    for side in (0, 1):
+        cand_copy(side).wait_recv()
+    same = jnp.full((32, 3584), owner, jnp.int32) == c + 1 - 2 * k
+    chosen = jnp.where(same, cand[0].astype(F32), cand[1].astype(F32)).astype(BF16)
+    stacked = jnp.concatenate([chosen[:, g * 896 : (g + 1) * 896] for g in range(4)], axis=0)
+    turned = nt(stacked, pick).astype(BF16)
+    for g in range(4):
+        for t in range(4):
+            encs[g // 2, t, :, (g % 2) * 256 : (g % 2) * 256 + 256] = turned[
+                g * 32 : (g + 1) * 32, t * 256 : (t + 1) * 256
+            ]
+
+    def ex_copy(d):
+        a, b, e = ppeer(d)
+        return remote(
+            encs.at[a, b * 2 + e], encb.at[h, b_me], ex_s.at[d], ex_r.at[b_me],
+            at(cid(a, z, b), h, e),
+        )
+
+    def ex_arrived(d):
+        i = bid(*ppeer(d))
+        remote(encb.at[h, i], encb.at[h, i], ex_s.at[d], ex_r.at[i], here).wait_recv()
+
+    def ey_copy(j):
+        hd = lax.rem(h + j, NH)
+        return remote(encb.at[h], encb.at[h], ey_s.at[hd], ey_r.at[h], at(c, hd, v))
+
+    def ey_arrived(j):
+        hs = lax.rem(h + j, NH)
+        remote(encb.at[hs], encb.at[hs], ey_s.at[hs], ey_r.at[hs], here).wait_recv()
+
+    each(1, 8, lambda d: ex_copy(d).start())
+    encb[h, b_me] = encs[xh, k * 2 + v]
     each(1, NZ, st_arrived)
     tops, totals, inners = st[:, 0:4, :], st[:, 4:8, :], st[:, 8:12, :]
     upper = jnp.max(tops, axis=0)
@@ -276,18 +307,17 @@
         zs = zpeer(j)
         remote(dqp.at[zs], dqr.at[zs], dq_s.at[zs], dq_r.at[zs], here).wait_recv()
 
-    each(1, NZ, lambda j: dq_copy(j).start())
+    far_first(lambda j: dq_copy(j).start())
+    each(1, 8, ex_arrived)
+    each(1, NH, lambda j: ey_copy(j).start())
+    each(1, NH, w_forward)
     each(1, 4, rs_arrived)
     mine = dkvf[own4]
     for d in range(1, 4):
         a, b = kv_peer(d)
         mine = mine + dkvr[a * 2 + b].astype(F32)
     mine = mine.astype(BF16)
-    owner = own_ref[0, 0]
-    b_me = bid(xh, k, v)
-    to_same = jnp.where(jnp.full((16, 256), owner, jnp.int32) == c + 1 - 2 * k, 1.0, 0.0)
-    dkvg[b_me, 0:128, :] = mine
-    dkvg[b_me, 128:144, :] = to_same.astype(BF16)
+    dkvg[b_me] = mine
     hg[h] = mine
 
     def gx_peer(d):
@@ -325,15 +355,36 @@
 
     each(1, 4, forward)
 
+    def gc_arrived(d):
+        a, e = gx_peer(d)
+        i = bid(a, ko, e)
+        remote(dkvg.at[i], dkvg.at[i], gc_s.at[a * 2 + e], gc_r.at[a * 2 + e], here).wait_recv()
+
+    each(0, 4, gc_arrived)
+    each(1, NH, ey_arrived)
+    grads = jnp.concatenate(
+        [dkvg[i, n * 32 : (n + 1) * 32, :] for n in range(NH) for i in range(8)], axis=0
+    )
+    acc = tn(encb[...].reshape(1024, 512), grads)
+    for t in range(NZ):
+        first = (t // 4) * 256 + (t % 4) * PIECE
+        wgs[t] = acc[first : first + 64].astype(BF16)
+
+    def wg_copy(j):
+        zd = zpeer(j)
+        return remote(wgs.at[zd], wgr.at[z], wg_s.at[zd], wg_r.at[z], at(cid(xh, zd, k), h, v))
+
+    def wg_arrived(j):
+        zs = zpeer(j)
+        remote(wgs.at[zs], wgr.at[zs], wg_s.at[zs], wg_r.at[zs], here).wait_recv()
+
+    far_first(lambda j: wg_copy(j).start())
+
     def h_arrived(j):
         hs = lax.rem(h + j, NH)
         remote(hg.at[hs], hg.at[hs], h_s.at[hs], h_r.at[hs], here).wait_recv()
 
-    def w_arrived(j):
-        hs = lax.rem(h + j, NH)
-        remote(w_ref.at[wrows], wb.at[hs], w_s.at[hs], w_r.at[hs], here).wait_recv()
-
-    loads[5].wait()
+    loads[4].wait()
     each(1, NH, w_arrived)
     each(1, NH, h_arrived)
     summed = jnp.zeros((BLK, 896), F32)
@@ -351,45 +402,6 @@
     out_next.start()
     out_prev.start()
 
-    def gc_arrived(d):
-        a, e = gx_peer(d)
-        i = bid(a, ko, e)
-        remote(dkvg.at[i], dkvg.at[i], gc_s.at[a * 2 + e], gc_r.at[a * 2 + e], here).wait_recv()
-
-    def enc_arrived(side, a, b, e):
-        i = bid(a, b, e)
-        remote(
-            enct.at[0, 0, 0], encb.at[i, :, lanes(side)], e_s.at[side, 0], e_r.at[side, i], here
-        ).wait_recv()
-
-    def same_arrived(d):
-        a, b, e = ppeer(d)
-        enc_arrived(0, a, 1 - b, e)
-
-    each(0, 4, gc_arrived)
-    enc_own.wait()
-    each(1, 8, same_arrived)
-    each(0, 8, lambda d: enc_arrived(1, *ppeer(d)))
-    acc = jnp.zeros((512, 256), F32)
-    for i in range(8):
-        grads = dkvg[i, 0:128, :].astype(F32)
-        flag = dkvg[i, 128:144, :].astype(F32)[0:1, :]
-        both = jnp.concatenate([grads * flag, grads * (1.0 - flag)], axis=0).astype(BF16)
-        acc = acc + jnp.dot(encb[i], both, preferred_element_type=F32)
-    for t in range(NZ):
-        first = (t // 4) * 256 + (t % 4) * PIECE
-        wgs[t] = acc[first : first + 64].astype(BF16)
-
-    def wg_copy(j):
-        zd = zpeer(j)
-        return remote(wgs.at[zd], wgr.at[z], wg_s.at[zd], wg_r.at[z], at(cid(xh, zd, k), h, v))
-
-    def wg_arrived(j):
-        zs = zpeer(j)
-        remote(wgs.at[zs], wgr.at[zs], wg_s.at[zs], wg_r.at[zs], here).wait_recv()
-
-    each(1, NZ, lambda j: wg_copy(j).start())
-
     each(1, NZ, dq_arrived)
     query_grad = dqp[z].astype(F32)
     for j in range(1, NZ):
@@ -399,26 +411,30 @@
         [query_grad[g * 8 : (g + 1) * 8] for g in range(QPG)], axis=1
     ).astype(BF16)
 
-    each(1, NZ, wg_arrived)
-    weight = wgs[z].astype(F32)
-    for j in range(1, NZ):
-        weight = weight + wgr[zpeer(j)].astype(F32)
-    wg_ref[...] = weight[:PIECE]
-
-    out_next.wait_recv()
-    out_prev.wait_recv()
     each(1, NZ, lambda j: q_copy(j).wait_send())
     for side in (0, 1):
         each(1, 4, lambda d: kv_copy(d, side).wait_send())
+    for side in (0, 1):
+        cand_copy(side).wait_send()
     each(1, NH, lambda j: w_copy(j).wait_send())
-    each(1, 8, lambda d: enc_same(d).wait_send())
-    each(0, 8, lambda d: enc_cross(d).wait_send())
+    each(1, NH, lambda j: w_pass(j).wait_send())
+    each(1, 8, lambda d: ex_copy(d).wait_send())
+    each(1, NH, lambda j: ey_copy(j).wait_send())
     each(1, NZ, lambda j: st_copy(j).wait_send())
     each(1, 4, lambda d: rs_copy(d).wait_send())
     each(1, NZ, lambda j: dq_copy(j).wait_send())
     each(1, 4, lambda d: gx_copy(d).wait_send())
     each(0, 4, lambda d: gc_copy(d).wait_send())
     each(1, NH, lambda j: h_copy(j).wait_send())
+
+    each(1, NZ, wg_arrived)
+    weight = wgs[z].astype(F32)
+    for j in range(1, NZ):
+        weight = weight + wgr[zpeer(j)].astype(F32)
+    wg_ref[...] = weight[:PIECE]
+
+    out_next.wait_recv()
+    out_prev.wait_recv()
     out_next.wait_send()
     out_prev.wait_send()
     each(1, NZ, lambda j: wg_copy(j).wait_send())
@@ -445,9 +461,9 @@
             vmem((NZ, 2, 64, HD), BF16),
             vmem((4, BLK, HD), BF16),
             vmem((4, BLK, HD), BF16),
-            vmem((256, 3584), BF16),
-            vmem((2, 2, 4, 512, 128), BF16),
-            vmem((8, 512, 256), BF16),
+            vmem((2, 32, 3584), BF16),
+            vmem((2, 4, 32, 512), BF16),
+            vmem((NH, 8, 32, 512), BF16),
             vmem((NH, 896, 256), BF16),
             vmem((NZ, 16, 128), F32),
             vmem((8, 128), F32),
@@ -456,14 +472,14 @@
             vmem((4, BLK, 256), BF16),
             vmem((4, BLK, 256), BF16),
             vmem((4, BLK, 256), F32),
-            vmem((8, 144, 256), BF16),
+            vmem((8, BLK, 256), BF16),
             vmem((NH, BLK, 256), BF16),
             vmem((NZ, 64, HD), BF16),
             vmem((NZ, 64, HD), BF16),
             vmem((2, BLK, 896), BF16),
             vmem((NZ, 64, 256), BF16),
             vmem((NZ, 64, 256), BF16),
-            dma((7,)),
+            dma((5,)),
             dma((NZ,)), dma((NZ,)),
             dma((2, 4)), dma((2, 4)),
             dma((NZ,)), dma((NZ,)),
@@ -471,7 +487,10 @@
             dma((4,)), dma((4,)),
             dma((4,)), dma((4,)),
             dma((4,)), dma((4,)),
-            dma((2, 8)), dma((2, 8)),
+            dma((2,)), dma((2,)),
+            dma((8,)), dma((8,)),
+            dma((NH,)), dma((NH,)),
+            dma((NH,)), dma((NH,)),
             dma((NH,)), dma((NH,)),
             dma((NH,)), dma((NH,)),
             dma((2,)), dma((2,)),

time: 72.4 us -> 60.9 us (0.84)
  Pallas kernels: 65.6 us -> 54 us
    pallas_call x1, Pallas kernels: 65.6 us -> 54 us  [per_device(): pl.pallas_call(kernel, out_shape=(jax.ShapeDtypeStruct((8, 896), BF16), j...]
where the time goes in v2:
time: 60.9 us; the launch traced here: 60.5 us
  Pallas kernels  54 us (89%)
  local copies, waits for them, and re-layouts  4.58 us (8%)
  between operations  1.93 us (3%)
    pallas_call x1, Pallas kernels, per_device(): pl.pallas_call(kernel, out_shape=(jax.ShapeDtypeStruct((8, 896), BF16), j...  54 us
    unnamed x3, local copies, waits for them, and re-layouts  4.58 us

profile of v2, /device:TPU:1, one launch (start us, length us, event | category | flops | bytes accessed | tf_op | source)
XLA Modules:
  0.0 60.5 jit_solution(13143921749343463617)
XLA Ops:
  1.9 54.0 %shard_map.103 = (bf16[8,896]{1,0:T(8,128)(2,1)}, bf16[256,896]{1,0:T(8,128)(2,1)}, f32[56,256]{1,0:T(8,128)}) custom-call(bf16[8,896]{1,0:T(8,128)(2,1)} %bitcast.11, bf16[128,128]{1,0:T(8,128)(2,1)} %bitcast.9, bf16[128,128]{1,0:T(8,128)(2,1)} %bitcast.10, bf16[8,896]{1,0:T(8,128)(2,1)} %bitcast.12, s32[1]{0:T(128)S(6)} %copy.14.len_ref, ...), custom_call_target="tpu_custom_call" | custom-call | tf_op jit(solution)/shard_map/pallas_call | solution.py:449
  55.9 1.3 %copy.16 = bf16[1,8,896]{2,1,0:T(8,128)(2,1)} copy(bf16[1,8,896]{2,1,0:T(8,128)(2,1)} %bitcast.13) | data formatting | bytes 28672
  57.2 1.8 %copy.17 = bf16[1,256,896]{2,1,0:T(8,128)(2,1)} copy(bf16[1,256,896]{2,1,0:T(8,128)(2,1)} %bitcast.8) | data formatting | bytes 917504
  59.0 1.4 %copy.18 = f32[56,256]{1,0:T(8,128)} copy(f32[56,256]{1,0:T(8,128)} %get-tuple-element.14) | data formatting | bytes 114688

commit v3 on v2

--- a/solution.py
+++ b/solution.py
@@ -36,9 +36,9 @@
 
 
 def kernel(
-    q_ref, k_ref, v_ref, do_ref, len_ref, own_ref, enc_ref, w_ref,
+    q_ref, k_ref, v_ref, do_ref, len_in, own_in, enc_ref, w_ref,
     dq_ref, eg_ref, wg_ref,
-    qv, dov, qg, kb, vb, cand, encs, encb, wb, st, cs, es, dp,
+    len_ref, own_ref, qv, dov, qg, kb, vb, cand, encs, encb, wb, st, cs, es, dp,
     dkvp, dkvr, dkvf, dkvg, hg, dqp, dqr, egs, wgs, wgr,
     lsem, q_s, q_r, kv_s, kv_r, st_s, st_r, dq_s, dq_r, rs_s, rs_r,
     gx_s, gx_r, gc_s, gc_r, c_s, c_r, ex_s, ex_r, ey_s, ey_r,
@@ -111,28 +111,18 @@
         pltpu.make_async_copy(k_ref, kb.at[own4], lsem.at[2]),
         pltpu.make_async_copy(v_ref, vb.at[own4], lsem.at[3]),
         pltpu.make_async_copy(w_ref.at[wrows], wb.at[h], lsem.at[4]),
+        pltpu.make_async_copy(len_in, len_ref, lsem.at[5]),
+        pltpu.make_async_copy(own_in, own_ref, lsem.at[6]),
     ]
     for load in loads:
         load.start()
     loads[0].wait()
     loads[1].wait()
-    pad = jnp.zeros((8, HD), F32)
-    for side, ref in ((0, qv), (1, dov)):
+    parts = []
+    for ref in (qv, dov):
         rows = ref[...].astype(F32)
-        parts = [rows[:, g * HD : (g + 1) * HD] for g in range(QPG)] + [pad]
-        qg[z, side] = jnp.concatenate(parts, axis=0).astype(BF16)
-
-    row = lax.broadcasted_iota(jnp.int32, (1024, 896), 0)
-    col = lax.broadcasted_iota(jnp.int32, (1024, 896), 1)
-    inner_row = lax.rem(row, 256)
-    quarter = lax.div(row, 256)
-    step_of = (
-        (inner_row >= PIECE).astype(jnp.int32)
-        + (inner_row >= 2 * PIECE).astype(jnp.int32)
-        + (inner_row >= 3 * PIECE).astype(jnp.int32)
-    )
-    source = step_of * (4 * PIECE) + quarter * PIECE + inner_row - step_of * PIECE
-    pick = jnp.where((col == source) & (inner_row < 4 * PIECE), 1.0, 0.0).astype(BF16)
+        parts += [rows[:, g * HD : (g + 1) * HD] for g in range(QPG)]
+    qg[z] = jnp.concatenate(parts, axis=0).astype(BF16)
 
     pl.semaphore_wait(barrier, 18)
 
@@ -201,11 +191,19 @@
 
     loads[2].wait()
     loads[3].wait()
+    loads[5].wait()
+    loads[6].wait()
     each(1, 4, kv_arrived)
     each(1, NZ, q_arrived)
     keys = kb[...].reshape(512, HD)
-    queries = qg[:, 0].reshape(512, HD)
-    dout = qg[:, 1].reshape(512, HD)
+    text = qg[...].astype(F32)
+    rest = jnp.zeros((512 - NZ * PIECE, HD), F32)
+
+    def text_rows(first):
+        rows = text[:, first : first + PIECE].reshape(NZ * PIECE, HD)
+        return jnp.concatenate([rows, rest], axis=0).astype(BF16)
+
+    queries, dout = text_rows(0), text_rows(PIECE)
     block = lax.div(lax.broadcasted_iota(jnp.int32, (512, 512), 0), BLK)
     place = lax.div(block, 2) * (2 * NZ) + z * 2 + lax.rem(block, 2)
     valid = place < len_ref[0]
@@ -233,17 +231,16 @@
 
     owner = own_ref[0, 0]
     b_me = bid(xh, k, v)
-    for side in (0, 1):
-        cand_copy(side).wait_recv()
+    cand_copy(0).wait_recv()
+    cand_copy(1).wait_recv()
     same = jnp.full((32, 3584), owner, jnp.int32) == c + 1 - 2 * k
-    chosen = jnp.where(same, cand[0].astype(F32), cand[1].astype(F32)).astype(BF16)
-    stacked = jnp.concatenate([chosen[:, g * 896 : (g + 1) * 896] for g in range(4)], axis=0)
-    turned = nt(stacked, pick).astype(BF16)
-    for g in range(4):
+    chosen = jnp.where(same, cand[0].astype(F32), cand[1].astype(F32))
+    blank = jnp.zeros((32, 512 - NZ * PIECE), F32)
+    for a in (0, 1):
         for t in range(4):
-            encs[g // 2, t, :, (g % 2) * 256 : (g % 2) * 256 + 256] = turned[
-                g * 32 : (g + 1) * 32, t * 256 : (t + 1) * 256
-            ]
+            starts = [a * 1792 + n * 4 * PIECE + t * PIECE for n in range(NZ)]
+            pieces = [chosen[:, first : first + PIECE] for first in starts]
+            encs[a, t] = jnp.concatenate(pieces + [blank], axis=1).astype(BF16)
 
     def ex_copy(d):
         a, b, e = ppeer(d)
@@ -256,13 +253,23 @@
         i = bid(*ppeer(d))
         remote(encb.at[h, i], encb.at[h, i], ex_s.at[d], ex_r.at[i], here).wait_recv()
 
-    def ey_copy(j):
-        hd = lax.rem(h + j, NH)
-        return remote(encb.at[h], encb.at[h], ey_s.at[hd], ey_r.at[h], at(c, hd, v))
-
-    def ey_arrived(j):
-        hs = lax.rem(h + j, NH)
-        remote(encb.at[hs], encb.at[hs], ey_s.at[hs], ey_r.at[hs], here).wait_recv()
+    up, down, far = lax.rem(h + 1, NH), lax.rem(h + 3, NH), lax.rem(h + 2, NH)
+
+    def ey_copy(side):
+        hd = (up, down)[side]
+        return remote(encb.at[h], encb.at[h], ey_s.at[side], ey_r.at[side], at(c, hd, v))
+
+    def ey_arrived(side):
+        hs = (down, up)[side]
+        remote(encb.at[hs], encb.at[hs], ey_s.at[side], ey_r.at[side], here).wait_recv()
+
+    def ey_pass(side):
+        part = encb.at[(down, up)[side], pl.ds(4 * side, 4)]
+        return remote(part, part, ey_s.at[2 + side], ey_r.at[2 + side], at(c, (up, down)[side], v))
+
+    def ey_passed(side):
+        part = encb.at[far, pl.ds(4 * side, 4)]
+        remote(part, part, ey_s.at[2 + side], ey_r.at[2 + side], here).wait_recv()
 
     each(1, 8, lambda d: ex_copy(d).start())
     encb[h, b_me] = encs[xh, k * 2 + v]
@@ -297,7 +304,9 @@
 
     each(1, 4, lambda d: rs_copy(d).start())
 
-    dqp[...] = tn(score_low, keys).reshape(NZ, 64, HD).astype(BF16)
+    query_part = tn(score_low, keys)
+    for t in range(NZ):
+        dqp[t] = query_part[t * PIECE : t * PIECE + 64].astype(BF16)
 
     def dq_copy(j):
         zd = zpeer(j)
@@ -309,7 +318,8 @@
 
     far_first(lambda j: dq_copy(j).start())
     each(1, 8, ex_arrived)
-    each(1, NH, lambda j: ey_copy(j).start())
+    ey_copy(0).start()
+    ey_copy(1).start()
     each(1, NH, w_forward)
     each(1, 4, rs_arrived)
     mine = dkvf[own4]
@@ -353,32 +363,11 @@
         ).wait_recv()
         gc_copy(d).start()
 
+    ey_arrived(0)
+    ey_pass(0).start()
+    ey_arrived(1)
+    ey_pass(1).start()
     each(1, 4, forward)
-
-    def gc_arrived(d):
-        a, e = gx_peer(d)
-        i = bid(a, ko, e)
-        remote(dkvg.at[i], dkvg.at[i], gc_s.at[a * 2 + e], gc_r.at[a * 2 + e], here).wait_recv()
-
-    each(0, 4, gc_arrived)
-    each(1, NH, ey_arrived)
-    grads = jnp.concatenate(
-        [dkvg[i, n * 32 : (n + 1) * 32, :] for n in range(NH) for i in range(8)], axis=0
-    )
-    acc = tn(encb[...].reshape(1024, 512), grads)
-    for t in range(NZ):
-        first = (t // 4) * 256 + (t % 4) * PIECE
-        wgs[t] = acc[first : first + 64].astype(BF16)
-
-    def wg_copy(j):
-        zd = zpeer(j)
-        return remote(wgs.at[zd], wgr.at[z], wg_s.at[zd], wg_r.at[z], at(cid(xh, zd, k), h, v))
-
-    def wg_arrived(j):
-        zs = zpeer(j)
-        remote(wgs.at[zs], wgr.at[zs], wg_s.at[zs], wg_r.at[zs], here).wait_recv()
-
-    far_first(lambda j: wg_copy(j).start())
 
     def h_arrived(j):
         hs = lax.rem(h + j, NH)
@@ -402,6 +391,32 @@
     out_next.start()
     out_prev.start()
 
+    def gc_arrived(d):
+        a, e = gx_peer(d)
+        i = bid(a, ko, e)
+        remote(dkvg.at[i], dkvg.at[i], gc_s.at[a * 2 + e], gc_r.at[a * 2 + e], here).wait_recv()
+
+    each(0, 4, gc_arrived)
+    ey_passed(0)
+    ey_passed(1)
+    grads = jnp.concatenate(
+        [dkvg[i, n * 32 : (n + 1) * 32, :] for n in range(NH) for i in range(8)], axis=0
+    )
+    acc = tn(encb[...].reshape(1024, 512), grads)
+    for t in range(NZ):
+        piece = acc[t * PIECE : (t + 1) * PIECE]
+        wgs[t] = jnp.concatenate([piece[:, :128], piece[:, 128:]], axis=0).astype(BF16)
+
+    def wg_copy(j):
+        zd = zpeer(j)
+        return remote(wgs.at[zd], wgr.at[z], wg_s.at[zd], wg_r.at[z], at(cid(xh, zd, k), h, v))
+
+    def wg_arrived(j):
+        zs = zpeer(j)
+        remote(wgs.at[zs], wgr.at[zs], wg_s.at[zs], wg_r.at[zs], here).wait_recv()
+
+    far_first(lambda j: wg_copy(j).start())
+
     each(1, NZ, dq_arrived)
     query_grad = dqp[z].astype(F32)
     for j in range(1, NZ):
@@ -419,7 +434,9 @@
     each(1, NH, lambda j: w_copy(j).wait_send())
     each(1, NH, lambda j: w_pass(j).wait_send())
     each(1, 8, lambda d: ex_copy(d).wait_send())
-    each(1, NH, lambda j: ey_copy(j).wait_send())
+    for side in (0, 1):
+        ey_copy(side).wait_send()
+        ey_pass(side).wait_send()
     each(1, NZ, lambda j: st_copy(j).wait_send())
     each(1, 4, lambda d: rs_copy(d).wait_send())
     each(1, NZ, lambda j: dq_copy(j).wait_send())
@@ -431,7 +448,7 @@
     weight = wgs[z].astype(F32)
     for j in range(1, NZ):
         weight = weight + wgr[zpeer(j)].astype(F32)
-    wg_ref[...] = weight[:PIECE]
+    wg_ref[...] = jnp.concatenate([weight[:PIECE], weight[PIECE:]], axis=1)
 
     out_next.wait_recv()
     out_prev.wait_recv()
@@ -440,25 +457,48 @@
     each(1, NZ, lambda j: wg_copy(j).wait_send())
 
 
+def copy_kernel(dq_in, eg_in, wg_in, dq_out, eg_out, wg_out, sems):
+    pairs = ((dq_in, dq_out), (eg_in, eg_out), (wg_in, wg_out))
+    moves = [pltpu.make_async_copy(a, b, sems.at[i]) for i, (a, b) in enumerate(pairs)]
+    for move in moves:
+        move.start()
+    for move in moves:
+        move.wait()
+
+
+def finish(dq, eg, wg):
+    hbm = pl.BlockSpec(memory_space=pl.ANY)
+    arrays = tuple(pltpu.with_memory_space_constraint(a, pltpu.VMEM) for a in (dq, eg, wg))
+    outs = pl.pallas_call(
+        copy_kernel,
+        out_shape=tuple(jax.ShapeDtypeStruct(a.shape, a.dtype) for a in arrays),
+        in_specs=[pl.BlockSpec(memory_space=pltpu.VMEM)] * 3,
+        out_specs=(hbm,) * 3,
+        scratch_shapes=[pltpu.SemaphoreType.DMA((3,))],
+    )(*arrays)
+    return outs[0][None], outs[1][None], outs[2]
+
+
 def per_device(queries, keys, values, dout, lengths, owner, enc_rows, w_kv):
     dma = pltpu.SemaphoreType.DMA
     vmem = pltpu.VMEM
     hbm = pl.BlockSpec(memory_space=pl.ANY)
-    smem = pl.BlockSpec(memory_space=pltpu.SMEM)
     out = pl.BlockSpec(memory_space=pltpu.VMEM)
     dq, eg, wg = pl.pallas_call(
         kernel,
         out_shape=(
-            jax.ShapeDtypeStruct((8, 896), BF16),
-            jax.ShapeDtypeStruct((256, 896), BF16),
-            jax.ShapeDtypeStruct((PIECE, 256), F32),
+            vmem((8, 896), BF16),
+            vmem((256, 896), BF16),
+            vmem((PIECE, 256), F32),
         ),
-        in_specs=[hbm, hbm, hbm, hbm, smem, smem, hbm, hbm],
-        out_specs=(out, hbm, out),
+        in_specs=[hbm] * 8,
+        out_specs=(out, out, out),
         scratch_shapes=[
+            pltpu.SMEM((1,), jnp.int32),
+            pltpu.SMEM((1, 1), jnp.int32),
             vmem((8, 896), BF16),
             vmem((8, 896), BF16),
-            vmem((NZ, 2, 64, HD), BF16),
+            vmem((NZ, 2 * PIECE, HD), BF16),
             vmem((4, BLK, HD), BF16),
             vmem((4, BLK, HD), BF16),
             vmem((2, 32, 3584), BF16),
@@ -477,9 +517,9 @@
             vmem((NZ, 64, HD), BF16),
             vmem((NZ, 64, HD), BF16),
             vmem((2, BLK, 896), BF16),
-            vmem((NZ, 64, 256), BF16),
-            vmem((NZ, 64, 256), BF16),
-            dma((5,)),
+            vmem((NZ, 2 * PIECE, 128), BF16),
+            vmem((NZ, 2 * PIECE, 128), BF16),
+            dma((7,)),
             dma((NZ,)), dma((NZ,)),
             dma((2, 4)), dma((2, 4)),
             dma((NZ,)), dma((NZ,)),
@@ -500,7 +540,7 @@
             collective_id=0, has_side_effects=True, vmem_limit_bytes=60 * 1024 * 1024
         ),
     )(queries[0], keys[0], values[0], dout[0], lengths, owner, enc_rows[0], w_kv)
-    return dq[None], eg[None], wg
+    return finish(dq, eg, wg)
 
 
 def solution(mesh):

time: 60.9 us -> 51.7 us (0.85)
  local copies, waits for them, and re-layouts: 4.58 us -> 0 us
  Pallas kernels: 54 us -> 49.6 us
    unnamed x3 -> x0, local copies, waits for them, and re-layouts: 4.58 us -> none
    pallas_call x1 -> x2, Pallas kernels: 54 us -> 49.6 us  [the longest x1 48.8 us: per_device(): pl.pallas_call(kernel, out_shape=(vmem((8, 896), BF16), vmem((256, 896),...]
where the time goes in v3:
time: 51.7 us; the launch traced here: 51.5 us
  Pallas kernels  49.6 us (96%)
  between operations  1.93 us (4%)
    pallas_call x1, Pallas kernels, per_device(): pl.pallas_call(kernel, out_shape=(vmem((8, 896), BF16), vmem((256, 896),...  48.8 us

profile of v3, /device:TPU:1, one launch (start us, length us, event | category | flops | bytes accessed | tf_op | source)
XLA Modules:
  0.0 51.5 jit_solution(4765632942082665838)
XLA Ops:
  1.9 48.8 %shard_map.103 = (bf16[8,896]{1,0:T(8,128)(2,1)S(1)}, bf16[256,896]{1,0:T(8,128)(2,1)S(1)}, f32[56,256]{1,0:T(8,128)S(1)}) custom-call(bf16[8,896]{1,0:T(8,128)(2,1)} %bitcast.10, bf16[128,128]{1,0:T(8,128)(2,1)} %bitcast.8, bf16[128,128]{1,0:T(8,128)(2,1)} %bitcast.9, bf16[8,896]{1,0:T(8,128)(2,1)} %bitcast.11, s32[1]{0:T(128)S(6)} %copy.11.len_in, ...), custom_call_target="tpu_custom_call" | custom-call | tf_op jit(solution)/shard_map/pallas_call | solution.py:487
  50.7 0.8 %shard_map.104 = (bf16[8,896]{1,0:T(8,128)(2,1)}, bf16[256,896]{1,0:T(8,128)(2,1)}, f32[56,256]{1,0:T(8,128)}) custom-call(bf16[8,896]{1,0:T(8,128)(2,1)S(1)} %get-tuple-element.9.dq_in, bf16[256,896]{1,0:T(8,128)(2,1)S(1)} %get-tuple-element.10.eg_in, f32[56,256]{1,0:T(8,128)S(1)} %get-tuple-element.11.wg_in), custom_call_target="tpu_custom_call" | custom-call | tf_op jit(solution)/shard_map/pallas_call | solution.py:472

commit v4 on v3

v4 whole, which is shorter than its diff:
```python
import math

import jax
import jax.numpy as jnp
from jax import lax
from jax.experimental import pallas as pl
from jax.experimental.pallas import tpu as pltpu
from jax.sharding import PartitionSpec as P

NZ = 8
NC = 32
NH = 4
HD = 128
BLK = 128
QPG = 7
PIECE = 56
F32 = jnp.float32
BF16 = jnp.bfloat16
MESH = pl.DeviceIdType.MESH


SEMS = (
    "q", "k", "w", "small", "q_s", "q_r", "k_s", "k_r", "v_s", "v_r", "st_s", "st_r",
    "dq_s", "dq_r", "rs_s", "rs_r", "gx_s", "gc_s", "gc_r", "c_s", "c_r", "ex_s",
    "eu_s", "ed_s", "ep_s", "ep_r", "w_s", "w_r", "wf_s", "wf_r", "h_s",
    "o_s", "o_r", "wg_s", "wg_r", "do", "v", "own",
)


def each(start, stop, fn):
    def step(i, carry):
        fn(i)
        return carry

    lax.fori_loop(start, stop, step, 0)


def nt(a, b):
    return lax.dot_general(a, b, (((1,), (1,)), ((), ())), preferred_element_type=F32)


def tn(a, b):
    return lax.dot_general(a, b, (((0,), (0,)), ((), ())), preferred_element_type=F32)


def kernel(
    q_ref, k_ref, v_ref, do_ref, len_in, own_in, enc_ref, w_ref,
    dq_ref, eg_ref, wg_ref,
    len_ref, own_ref, qv, dov, qg, kb, vb, cand, encs, encb, wb, st, cs, es, dp,
    dkvp, dkvr, dkvf, dkvg, hg, dqp, dqr, egs, wgs, wgr,
    terms_sum, sems, gx_r, ex_r, ey_r, h_r,
):
    factor = 1.0 / math.sqrt(HD)
    c = lax.axis_index("ctx")
    h = lax.axis_index("head")
    v = lax.axis_index("video")
    xh, z, k = lax.div(c, 2 * NZ), lax.rem(lax.div(c, 2), NZ), lax.rem(c, 2)
    ko = 1 - k
    c_next, c_prev = lax.rem(c + 1, NC), lax.rem(c + NC - 1, NC)
    c_cross = lax.rem(c + 2 * k - 1 + NC, NC)

    def cid(a, b, d):
        return (a * NZ + b) * 2 + d

    def at(ctx, head, video):
        return {"ctx": ctx, "head": head, "video": video}

    def remote(src, dst, ssem, rsem, dev):
        return pltpu.make_async_remote_copy(
            src_ref=src, dst_ref=dst, send_sem=ssem, recv_sem=rsem,
            device_id=dev, device_id_type=MESH,
        )

    here = at(c, h, v)

    def sent(ref, name):
        remote(ref, ref, sem(name + "_s"), sem(name + "_s"), here).wait_send()

    def arrived(ref, name):
        remote(ref, ref, sem(name + "_r"), sem(name + "_r"), here).wait_recv()

    def sem(name):
        return sems.at[SEMS.index(name)]

    def zpeer(j):
        return lax.rem(z + j, NZ)

    def far_first(fn):
        def step(i):
            half = lax.div(i + 1, 2)
            fn(4 + half - 2 * half * lax.rem(i, 2))

        each(0, NZ - 1, step)

    def ppeer(d):
        return (
            lax.rem(xh + lax.div(d, 4), 2),
            lax.rem(k + lax.rem(lax.div(d, 2), 2), 2),
            lax.rem(v + lax.rem(d, 2), 2),
        )

    def bid(a, b, d):
        return a * 4 + d * 2 + b

    barrier = pltpu.get_barrier_semaphore()

    def signal(dev):
        pl.semaphore_signal(barrier, inc=1, device_id=dev, device_id_type=MESH)

    each(1, NZ, lambda j: signal(at(cid(xh, zpeer(j), k), h, v)))

    def sig_plane(d):
        a, b, e = ppeer(d)
        signal(at(cid(a, z, b), h, e))

    each(1, 8, sig_plane)

    signal(at(c_cross, h, v))
    each(1, NH, lambda j: signal(at(c, lax.rem(h + j, NH), v)))

    own4 = xh * 2 + k
    wrows = pl.ds(pl.multiple_of(h * 896, 128), 896)
    loads = [
        pltpu.make_async_copy(q_ref, qv, sem("q")),
        pltpu.make_async_copy(do_ref, dov, sem("do")),
        pltpu.make_async_copy(k_ref, kb.at[own4], sem("k")),
        pltpu.make_async_copy(v_ref, vb.at[own4], sem("v")),
        pltpu.make_async_copy(w_ref.at[wrows], wb.at[wrows], sem("w")),
        pltpu.make_async_copy(len_in, len_ref, sem("small")),
        pltpu.make_async_copy(own_in, own_ref, sem("own")),
    ]
    for load in loads:
        load.start()
    loads[0].wait()
    loads[1].wait()
    parts = []
    for ref in (qv, dov):
        rows = ref[...].astype(F32)
        parts += [rows[:, g * HD : (g + 1) * HD] for g in range(QPG)]
    qg[z] = jnp.concatenate(parts, axis=0).astype(BF16)

    pl.semaphore_wait(barrier, 18)

    def q_copy(j):
        zd = zpeer(j)
        return remote(qg.at[z], qg.at[z], sem("q_s"), sem("q_r"), at(cid(xh, zd, k), h, v))

    far_first(lambda j: q_copy(j).start())

    def kv_peer(d):
        return lax.rem(xh + lax.div(d, 2), 2), lax.rem(k + lax.rem(d, 2), 2)

    def kv_copy(d, side):
        a, b = kv_peer(d)
        src, dst = ((k_ref, kb), (v_ref, vb))[side]
        name = ("k", "v")[side]
        return remote(
            src, dst.at[own4], sem(name + "_s"), sem(name + "_r"), at(cid(a, z, b), h, v)
        )

    for side in (0, 1):
        each(1, 4, lambda d: kv_copy(d, side).start())

    def cand_copy(side):
        slot, ctx = ((ko, cid(xh, z, ko)), (k, c_cross))[side]
        rows = pl.ds(pl.multiple_of(slot * BLK + h * 32, 32), 32)
        return remote(enc_ref.at[rows], cand.at[side], sem("c_s"), sem("c_r"), at(ctx, h, v))

    cand_copy(0).start()
    cand_copy(1).start()

    def w_rows(hd, core):
        return pl.ds(pl.multiple_of(hd * 896 + core * 448, 64), 448)

    def w_copy(j):
        hd = lax.rem(h + j, NH)
        return remote(
            w_ref.at[w_rows(hd, k)], wb.at[w_rows(h, k)], sem("w_s"), sem("w_r"), at(c, hd, v)
        )

    def w_pass(j):
        part = wb.at[w_rows(lax.rem(h + j, NH), k)]
        return remote(part, part, sem("wf_s"), sem("wf_r"), at(cid(xh, z, ko), h, v))

    three_halves = wb.at[pl.ds(0, 3 * 448)]
    each(1, NH, lambda j: w_copy(j).start())

    loads[2].wait()
    loads[3].wait()
    loads[5].wait()
    loads[6].wait()
    arrived(kb.at[pl.ds(0, 3)], "k")
    arrived(vb.at[pl.ds(0, 3)], "v")
    arrived(qg.at[pl.ds(0, 7)], "q")
    keys = kb[...].reshape(512, HD)
    text = qg[...].astype(F32)
    rest = jnp.zeros((512 - NZ * PIECE, HD), F32)

    def text_rows(first):
        rows = text[:, first : first + PIECE].reshape(NZ * PIECE, HD)
        return jnp.concatenate([rows, rest], axis=0).astype(BF16)

    queries, dout = text_rows(0), text_rows(PIECE)
    block = lax.div(lax.broadcasted_iota(jnp.int32, (512, 512), 0), BLK)
    place = lax.div(block, 2) * (2 * NZ) + z * 2 + lax.rem(block, 2)
    valid = place < len_ref[0]
    masked = jnp.where(valid, nt(keys, queries) * factor, -1e30)
    top = jnp.max(masked, axis=0, keepdims=True)
    terms = jnp.where(valid, jnp.exp(masked - top), 0.0)
    grad_prob = nt(vb[...].reshape(512, HD), dout)
    es[...] = terms
    dp[...] = grad_prob
    total = jnp.sum(terms, axis=0, keepdims=True)
    inner = jnp.sum(terms * grad_prob, axis=0, keepdims=True)
    for n, value in enumerate((top, total, inner)):
        for t in range(4):
            st[z, n * 4 + t : n * 4 + t + 1, :] = value[:, t * 128 : (t + 1) * 128]

    def st_copy(j):
        zd = zpeer(j)
        return remote(st.at[z], st.at[z], sem("st_s"), sem("st_r"), at(cid(xh, zd, k), h, v))

    far_first(lambda j: st_copy(j).start())

    owner = own_ref[0, 0]
    b_me = bid(xh, k, v)
    arrived(cand, "c")
    same = jnp.full((32, 3584), owner, jnp.int32) == c + 1 - 2 * k
    chosen = jnp.where(same, cand[0].astype(F32), cand[1].astype(F32))
    for a in (0, 1):
        for t in range(4):
            starts = [a * 1792 + n * 4 * PIECE + t * PIECE for n in range(NZ)]
            pieces = [
                chosen[first : first + 16, start : start + PIECE]
                for first in (0, 16)
                for start in starts
            ]
            encs[a, t] = jnp.concatenate(pieces, axis=1).astype(BF16)

    def ex_copy(d):
        a, b, e = ppeer(d)
        return remote(
            encs.at[a, b * 2 + e], encb.at[h, b_me], sem("ex_s"), ex_r.at[xh * 2 + v],
            at(cid(a, z, b), h, e),
        )

    up, down, far = lax.rem(h + 1, NH), lax.rem(h + 3, NH), lax.rem(h + 2, NH)

    def chip(i):
        return lax.rem(xh + i // 2, 2), lax.rem(v + ((i + 1) // 2) % 2, 2)

    def chunk(hd, i):
        if i < 2:
            return encb.at[hd, pl.ds(bid(xh, (k, ko)[i], v), 1)]
        a, e = chip(i - 1)
        return encb.at[hd, pl.ds(bid(a, 0, e), 2)]

    def ey_copy(side, i):
        part = chunk(h, i)
        return remote(
            part, part, sem(("eu_s", "ed_s")[side]), ey_r.at[side, i], at(c, (up, down)[side], v)
        )

    def ey_arrived(side, i):
        part = chunk((down, up)[side], i)
        remote(part, part, sem("eu_s"), ey_r.at[side, i], here).wait_recv()

    def ey_send(i):
        if i > 0:
            a, e = chip(i - 1)
            part = chunk(h, i)
            remote(part, part, sem("ex_s"), ex_r.at[a * 2 + e], here).wait_recv()
        ey_copy(0, i).start()
        if i not in (1, 2):
            ey_copy(1, i).start()

    def pass_side(i):
        return 0 if i < 3 else 1

    def ey_pass(i):
        side = pass_side(i)
        part = chunk((down, up)[side], i)
        return remote(part, part, sem("ep_s"), sem("ep_r"), at(c, (up, down)[side], v))

    def ey_relay(i):
        ey_arrived(pass_side(i), i)
        ey_pass(i).start()

    encb[h, b_me] = encs[xh, k * 2 + v]
    ey_send(0)
    for d in (2, 1, 3, 5, 7, 4, 6):
        ex_copy(d).start()
    arrived(st.at[pl.ds(0, 7)], "st")
    tops, totals, inners = st[:, 0:4, :], st[:, 4:8, :], st[:, 8:12, :]
    upper = jnp.max(tops, axis=0)
    scales = jnp.exp(tops - upper[None])
    sum_total = jnp.sum(totals * scales, axis=0)
    sum_inner = jnp.sum(inners * scales, axis=0)
    cs[0:4, :] = jnp.exp(st[z, 0:4, :] - upper) / sum_total
    cs[4:8, :] = sum_inner / sum_total
    scale = jnp.concatenate([cs[t : t + 1, :] for t in range(4)], axis=1)
    ratio = jnp.concatenate([cs[t : t + 1, :] for t in range(4, 8)], axis=1)
    attention = es[...] * scale
    score_low = (attention * (dp[...] - ratio)).astype(BF16)
    attention_low = attention.astype(BF16)
    key_grad = jnp.dot(score_low, queries, preferred_element_type=F32) * factor
    value_grad = jnp.dot(attention_low, dout, preferred_element_type=F32)
    key_value = jnp.concatenate([key_grad, value_grad], axis=1).reshape(4, BLK, 256)
    dkvf[...] = key_value
    dkvp[...] = key_value.astype(BF16)

    def rs_copy(d):
        a, b = kv_peer(d)
        i = a * 2 + b
        return remote(dkvp.at[i], dkvr.at[own4], sem("rs_s"), sem("rs_r"), at(cid(a, z, b), h, v))

    each(1, 4, lambda d: rs_copy(d).start())

    ey_send(1)

    query_part = tn(score_low, keys)
    for t in range(NZ):
        dqp[t] = query_part[t * PIECE : t * PIECE + 64].astype(BF16)

    def dq_copy(j):
        zd = zpeer(j)
        return remote(dqp.at[zd], dqr.at[z], sem("dq_s"), sem("dq_r"), at(cid(xh, zd, k), h, v))

    far_first(lambda j: dq_copy(j).start())
    ey_send(2)
    ey_send(3)
    ey_send(4)
    ey_copy(1, 1).start()
    ey_copy(1, 2).start()
    arrived(three_halves, "w")
    each(1, NH, lambda j: w_pass(j).start())
    ey_relay(0)
    arrived(dkvr.at[pl.ds(0, 3)], "rs")
    mine = dkvf[own4]
    for d in range(1, 4):
        a, b = kv_peer(d)
        mine = mine + dkvr[a * 2 + b].astype(F32)
    mine = mine.astype(BF16)
    dkvg[b_me] = mine
    hg[h] = mine

    def gx_peer(d):
        return lax.rem(xh + lax.div(d, 2), 2), lax.rem(v + lax.rem(d, 2), 2)

    def gx_copy(d):
        a, e = gx_peer(d)
        return remote(
            dkvg.at[b_me], dkvg.at[b_me], sem("gx_s"), gx_r.at[xh * 2 + v],
            at(cid(a, z, k), h, e),
        )

    def gc_copy(d):
        a, e = gx_peer(d)
        i = bid(a, k, e)
        return remote(
            dkvg.at[i], dkvg.at[i], sem("gc_s"), sem("gc_r"), at(cid(xh, z, ko), h, v)
        )

    def h_copy(j):
        hd = lax.rem(h + j, NH)
        return remote(hg.at[h], hg.at[h], sem("h_s"), h_r.at[h], at(c, hd, v))

    each(1, 4, lambda d: gx_copy(d).start())
    each(1, NH, lambda j: h_copy(j).start())
    gc_copy(0).start()

    def forward(d):
        a, e = gx_peer(d)
        i = bid(a, k, e)
        remote(
            dkvg.at[i], dkvg.at[i], sem("gx_s"), gx_r.at[a * 2 + e], here
        ).wait_recv()
        gc_copy(d).start()

    ey_relay(1)
    ey_relay(2)
    ey_relay(3)
    ey_relay(4)

    def head_term(n):
        rows = pl.ds(pl.multiple_of(n * 896, 128), 896)
        return nt(hg[n], wb[rows, :]).astype(BF16).astype(F32)

    def h_arrived(j):
        n = lax.rem(h + j, NH)
        remote(hg.at[n], hg.at[n], sem("h_s"), h_r.at[n], here).wait_recv()

    loads[4].wait()
    terms_sum[...] = head_term(h)
    each(1, 4, forward)

    arrived(three_halves, "wf")
    h_arrived(1)
    h_arrived(3)
    summed = terms_sum[...] + head_term(up) + head_term(down)
    h_arrived(2)
    summed = summed + head_term(far)
    owners = jnp.full((BLK, 896), owner, jnp.int32)
    egs[0] = jnp.where(owners == c_next, summed, 0.0).astype(BF16)
    egs[1] = jnp.where(owners == c_next, 0.0, summed).astype(BF16)
    out_next = remote(
        egs.at[0], eg_ref.at[pl.ds(0, 128)], sem("o_s"), sem("o_r"), at(c_next, h, v)
    )
    out_prev = remote(
        egs.at[1], eg_ref.at[pl.ds(128, 128)], sem("o_s"), sem("o_r"), at(c_prev, h, v)
    )
    out_next.start()
    out_prev.start()

    arrived(dkvg.at[pl.ds(0, 4)], "gc")
    for i in range(5):
        ey_arrived(1 - pass_side(i), i)

    def quarter(n):
        turned = encb[n].reshape(128, 896).T
        rows = jnp.concatenate([turned[:448], turned[448:]], axis=1)
        grads = jnp.concatenate(
            [
                dkvg[i, pl.ds(pl.multiple_of(n * 32 + first, 16), 16), :]
                for first in (0, 16)
                for i in range(8)
            ],
            axis=0,
        )
        return jnp.dot(rows, grads, preferred_element_type=F32)

    acc = quarter(h) + quarter(up) + quarter(down)
    arrived(encb.at[far], "ep")
    acc = acc + quarter(far)
    for t in range(NZ):
        piece = acc[t * PIECE : (t + 1) * PIECE]
        wgs[t] = jnp.concatenate([piece[:, :128], piece[:, 128:]], axis=0).astype(BF16)

    def wg_copy(j):
        zd = zpeer(j)
        return remote(wgs.at[zd], wgr.at[z], sem("wg_s"), sem("wg_r"), at(cid(xh, zd, k), h, v))

    far_first(lambda j: wg_copy(j).start())

    arrived(dqr.at[pl.ds(0, 7)], "dq")
    query_grad = dqp[z].astype(F32)
    for j in range(1, NZ):
        query_grad = query_grad + dqr[zpeer(j)].astype(F32)
    query_grad = query_grad * factor
    dq_ref[...] = jnp.concatenate(
        [query_grad[g * 8 : (g + 1) * 8] for g in range(QPG)], axis=1
    ).astype(BF16)

    sent(qg.at[pl.ds(0, 7)], "q")
    sent(kb.at[pl.ds(0, 3)], "k")
    sent(vb.at[pl.ds(0, 3)], "v")
    sent(cand, "c")
    sent(three_halves, "w")
    sent(three_halves, "wf")
    sent(encb.at[h, pl.ds(0, 7)], "ex")
    sent(encb.at[h], "eu")
    sent(encb.at[h], "ed")
    sent(encb.at[h], "ep")
    sent(st.at[pl.ds(0, 7)], "st")
    sent(dkvp.at[pl.ds(0, 3)], "rs")
    sent(dqp.at[pl.ds(0, 7)], "dq")
    sent(dkvg.at[pl.ds(0, 3)], "gx")
    sent(dkvg.at[pl.ds(0, 4)], "gc")
    sent(hg.at[pl.ds(0, 3)], "h")

    arrived(wgr.at[pl.ds(0, 7)], "wg")
    weight = wgs[z].astype(F32)
    for j in range(1, NZ):
        weight = weight + wgr[zpeer(j)].astype(F32)
    wg_ref[...] = jnp.concatenate([weight[:PIECE], weight[PIECE:]], axis=1)

    arrived(egs, "o")
    sent(egs, "o")
    sent(wgs.at[pl.ds(0, 7)], "wg")


def copy_kernel(dq_in, eg_in, wg_in, dq_out, eg_out, wg_out, sems):
    pairs = ((dq_in, dq_out), (eg_in, eg_out), (wg_in, wg_out))
    moves = [pltpu.make_async_copy(a, b, sems.at[i]) for i, (a, b) in enumerate(pairs)]
    for move in moves:
        move.start()
    for move in moves:
        move.wait()


def finish(dq, eg, wg):
    hbm = pl.BlockSpec(memory_space=pl.ANY)
    arrays = tuple(pltpu.with_memory_space_constraint(a, pltpu.VMEM) for a in (dq, eg, wg))
    outs = pl.pallas_call(
        copy_kernel,
        out_shape=tuple(jax.ShapeDtypeStruct(a.shape, a.dtype) for a in arrays),
        in_specs=[pl.BlockSpec(memory_space=pltpu.VMEM)] * 3,
        out_specs=(hbm,) * 3,
        scratch_shapes=[pltpu.SemaphoreType.DMA((3,))],
    )(*arrays)
    return outs[0][None], outs[1][None], outs[2]


def per_device(queries, keys, values, dout, lengths, owner, enc_rows, w_kv):
    dma = pltpu.SemaphoreType.DMA
    vmem = pltpu.VMEM
    hbm = pl.BlockSpec(memory_space=pl.ANY)
    out = pl.BlockSpec(memory_space=pltpu.VMEM)
    dq, eg, wg = pl.pallas_call(
        kernel,
        out_shape=(
            vmem((8, 896), BF16),
            vmem((256, 896), BF16),
            vmem((PIECE, 256), F32),
        ),
        in_specs=[hbm] * 8,
        out_specs=(out, out, out),
        scratch_shapes=[
            pltpu.SMEM((1,), jnp.int32),
            pltpu.SMEM((1, 1), jnp.int32),
            vmem((8, 896), BF16),
            vmem((8, 896), BF16),
            vmem((NZ, 2 * PIECE, HD), BF16),
            vmem((4, BLK, HD), BF16),
            vmem((4, BLK, HD), BF16),
            vmem((2, 32, 3584), BF16),
            vmem((2, 4, 16, 896), BF16),
            vmem((NH, 8, 16, 896), BF16),
            vmem((NH * 896, 256), BF16),
            vmem((NZ, 12, 128), F32),
            vmem((8, 128), F32),
            vmem((512, 512), F32),
            vmem((512, 512), F32),
            vmem((4, BLK, 256), BF16),
            vmem((4, BLK, 256), BF16),
            vmem((4, BLK, 256), F32),
            vmem((8, BLK, 256), BF16),
            vmem((NH, BLK, 256), BF16),
            vmem((NZ, 64, HD), BF16),
            vmem((NZ, 64, HD), BF16),
            vmem((2, BLK, 896), BF16),
            vmem((NZ, 2 * PIECE, 128), BF16),
            vmem((NZ, 2 * PIECE, 128), BF16),
            vmem((BLK, 896), F32),
            dma((len(SEMS),)),
            dma((4,)),
            dma((4,)),
            dma((2, 5)),
            dma((4,)),
        ],
        compiler_params=pltpu.CompilerParams(
            collective_id=0, has_side_effects=True, vmem_limit_bytes=60 * 1024 * 1024
        ),
    )(queries[0], keys[0], values[0], dout[0], lengths, owner, enc_rows[0], w_kv)
    return finish(dq, eg, wg)


def solution(mesh):
    placed = (
        P("video", "ctx", "head"),
        P("video", "ctx", "head"),
        P("video", "ctx", "head"),
        P("video", "ctx", "head"),
        P("video"),
        P("video", "ctx"),
        P("video", "ctx", None),
        P(None, "head"),
    )
    return jax.shard_map(
        per_device,
        mesh=mesh,
        in_specs=placed,
        out_specs=(
            P("video", "ctx", "head"),
            P("video", "ctx", "head"),
            P(("ctx", "video"), "head"),
        ),
        check_vma=False,
    )
```

time: 51.7 us -> 47.4 us (0.917)
  Pallas kernels: 49.6 us -> 45.3 us
    pallas_call x1, Pallas kernels: 48.8 us -> 44.5 us  [per_device(): pl.pallas_call(kernel, out_shape=(vmem((8, 896), BF16), vmem((256, 896),...]
where the time goes in v4:
time: 47.4 us; the launch traced here: 47.2 us
  Pallas kernels  45.3 us (96%)
  between operations  1.93 us (4%)
    pallas_call x1, Pallas kernels, per_device(): pl.pallas_call(kernel, out_shape=(vmem((8, 896), BF16), vmem((256, 896),...  44.5 us

profile of v4, /device:TPU:1, one launch (start us, length us, event | category | flops | bytes accessed | tf_op | source)
XLA Modules:
  0.0 47.2 jit_solution(17038060922180867724)
XLA Ops:
  1.9 44.5 %shard_map.103 = (bf16[8,896]{1,0:T(8,128)(2,1)S(1)}, bf16[256,896]{1,0:T(8,128)(2,1)S(1)}, f32[56,256]{1,0:T(8,128)S(1)}) custom-call(bf16[8,896]{1,0:T(8,128)(2,1)} %bitcast.10, bf16[128,128]{1,0:T(8,128)(2,1)} %bitcast.8, bf16[128,128]{1,0:T(8,128)(2,1)} %bitcast.9, bf16[8,896]{1,0:T(8,128)(2,1)} %bitcast.11, s32[1]{0:T(128)S(6)} %copy.11.len_in, ...), custom_call_target="tpu_custom_call" | custom-call | tf_op jit(solution)/shard_map/pallas_call | solution.py:509
  46.4 0.8 %shard_map.104 = (bf16[8,896]{1,0:T(8,128)(2,1)}, bf16[256,896]{1,0:T(8,128)(2,1)}, f32[56,256]{1,0:T(8,128)}) custom-call(bf16[8,896]{1,0:T(8,128)(2,1)S(1)} %get-tuple-element.9.dq_in, bf16[256,896]{1,0:T(8,128)(2,1)S(1)} %get-tuple-element.10.eg_in, f32[56,256]{1,0:T(8,128)S(1)} %get-tuple-element.11.wg_in), custom_call_target="tpu_custom_call" | custom-call | tf_op jit(solution)/shard_map/pallas_call | solution.py:494

commit v5 on v4

--- a/solution.py
+++ b/solution.py
@@ -147,6 +147,13 @@
 
     far_first(lambda j: q_copy(j).start())
 
+    def cand_copy(side):
+        slot, ctx = ((ko, cid(xh, z, ko)), (k, c_cross))[side]
+        rows = pl.ds(pl.multiple_of(slot * BLK + h * 32, 32), 32)
+        return remote(enc_ref.at[rows], cand.at[side], sem("c_s"), sem("c_r"), at(ctx, h, v))
+
+    cand_copy(1).start()
+
     def kv_peer(d):
         return lax.rem(xh + lax.div(d, 2), 2), lax.rem(k + lax.rem(d, 2), 2)
 
@@ -161,13 +168,7 @@
     for side in (0, 1):
         each(1, 4, lambda d: kv_copy(d, side).start())
 
-    def cand_copy(side):
-        slot, ctx = ((ko, cid(xh, z, ko)), (k, c_cross))[side]
-        rows = pl.ds(pl.multiple_of(slot * BLK + h * 32, 32), 32)
-        return remote(enc_ref.at[rows], cand.at[side], sem("c_s"), sem("c_r"), at(ctx, h, v))
-
     cand_copy(0).start()
-    cand_copy(1).start()
 
     def w_rows(hd, core):
         return pl.ds(pl.multiple_of(hd * 896 + core * 448, 64), 448)
@@ -440,7 +441,7 @@
         zd = zpeer(j)
         return remote(wgs.at[zd], wgr.at[z], sem("wg_s"), sem("wg_r"), at(cid(xh, zd, k), h, v))
 
-    far_first(lambda j: wg_copy(j).start())
+    each(1, NZ, lambda j: wg_copy(j).start())
 
     arrived(dqr.at[pl.ds(0, 7)], "dq")
     query_grad = dqp[z].astype(F32)

time: 47.4 us -> 47 us (level)
  no operation moved by 1% of the time
where the time goes in v5:
time: 47 us; the launch traced here: 46.8 us
  Pallas kernels  44.9 us (96%)
  between operations  1.93 us (4%)
    pallas_call x1, Pallas kernels, per_device(): pl.pallas_call(kernel, out_shape=(vmem((8, 896), BF16), vmem((256, 896),...  44.1 us

profile of v5, /device:TPU:1, one launch (start us, length us, event | category | flops | bytes accessed | tf_op | source)
XLA Modules:
  0.0 46.8 jit_solution(6708782948660233911)
XLA Ops:
  1.9 44.1 %shard_map.103 = (bf16[8,896]{1,0:T(8,128)(2,1)S(1)}, bf16[256,896]{1,0:T(8,128)(2,1)S(1)}, f32[56,256]{1,0:T(8,128)S(1)}) custom-call(bf16[8,896]{1,0:T(8,128)(2,1)} %bitcast.10, bf16[128,128]{1,0:T(8,128)(2,1)} %bitcast.8, bf16[128,128]{1,0:T(8,128)(2,1)} %bitcast.9, bf16[8,896]{1,0:T(8,128)(2,1)} %bitcast.11, s32[1]{0:T(128)S(6)} %copy.11.len_in, ...), custom_call_target="tpu_custom_call" | custom-call | tf_op jit(solution)/shard_map/pallas_call | solution.py:510
  46.0 0.8 %shard_map.104 = (bf16[8,896]{1,0:T(8,128)(2,1)}, bf16[256,896]{1,0:T(8,128)(2,1)}, f32[56,256]{1,0:T(8,128)}) custom-call(bf16[8,896]{1,0:T(8,128)(2,1)S(1)} %get-tuple-element.9.dq_in, bf16[256,896]{1,0:T(8,128)(2,1)S(1)} %get-tuple-element.10.eg_in, f32[56,256]{1,0:T(8,128)S(1)} %get-tuple-element.11.wg_in), custom_call_target="tpu_custom_call" | custom-call | tf_op jit(solution)/shard_map/pallas_call | solution.py:495
